TPU v7x, 512 devices: a whole 4x8x8 slice. The times are simulated.
512 devices in a mesh: graphs: 8 (over x, y_hi), dom: 64 (over y_lo, z, core).
Axes of the slice: x: 4, y: 8 (y_hi: 2, y_lo: 4; y = y_hi * 4 + y_lo), z: 8, core: 2. Of those that a mesh axis runs over, the one named last changes fastest.
Arguments:
- node_feats: float32 [65536, 256], P(('graphs', 'dom')), parts along dimension 0, may hold values from -6 to 6
- norm_gain: float32 [256], replicated, may hold values from 0.1 to 1.9
- w_query: bfloat16 [256, 256], replicated, may hold values from -32 to 32
- w_key: bfloat16 [256, 256], replicated, may hold values from -1 to 1
- w_value: bfloat16 [256, 256], replicated, may hold values from -0.375 to 0.375
- w_out: bfloat16 [256, 256], replicated, may hold values from -0.75 to 0.75
- msg_src_w: bfloat16 [256, 256], replicated, may hold values from -0.25 to 0.25
- msg_dst_w: bfloat16 [256, 256], replicated, may hold values from -0.25 to 0.25
- msg_bias: float32 [256], replicated, may hold values from -4 to 4
- msg_out_w: bfloat16 [256, 256], replicated, may hold values from -0.25 to 0.25
- msg_out_bias: float32 [256], replicated, may hold values from -3 to 3
- mlp_gain: float32 [256], replicated, may hold values from 0.1 to 1.9
- mlp_up: bfloat16 [256, 1024], replicated, may hold values from -0.375 to 0.375
- mlp_down: bfloat16 [1024, 256], replicated, may hold values from -0.1875 to 0.1875
- send_list: int32 [512, 64, 4], P(('graphs', 'dom')), parts along dimension 0, may hold values from 0 to 127
- send_count: int32 [512, 64], P('graphs', 'dom'), parts along dimension 0, may hold values from 0 to 4, as said below
- edge_src: int32 [512, 8, 128], P(('graphs', 'dom')), parts along dimension 0, may hold values from 0 to 383
- edge_dst: int32 [512, 8, 128], P(('graphs', 'dom')), parts along dimension 0, may hold values from 0 to 127
- edge_count: int32 [512], P(('graphs', 'dom')), parts along dimension 0, may hold values from 256 to 1024, as said below
Outputs:
- out_feats: float32 [65536, 256], P(('graphs', 'dom')), parts along dimension 0
There are 8 independent parts, one for each index of `graphs`. A program takes and returns all parts, laid end to end along the dimension named above; an argument that names none is the same for every part. Nothing has to cross between parts.
Inputs may be any that keep to these rules, and one draw needn't show every extreme that they name: `send_list`: entries in slots at or past the count are arbitrary local rows. `send_count`: some sender fills all 4 slots to some receiver. `edge_src`: slots below 128 are local nodes; slot 128 + p * 4 + j is slot j of the rows received from partition p. `edge_count`: live edge slots come first in a partition's order; some partition has all 1024 slots live.
All inputs are finite; a program needn't handle non-finite values.
Results may differ from a plain program's by a relative error of at most 0.0057.
Values may be sent and summed in bfloat16 or wider, within the bound.
No kernel may reach another device: no remote copies, remote signals or barrier semaphores. Data moves between devices by JAX's collectives and lax.ppermute only.
A program may use at most 64 MiB of HBM per device.

v0:
```python
import jax
import jax.numpy as jnp
from jax import lax
from jax.sharding import Mesh
from jax.sharding import PartitionSpec as P

HEADS = 8
DOM = ("dom_0", "dom_1", "dom_2")
GRAPHS_DOM = ("graphs", "dom_0", "dom_1", "dom_2")


def laid_out(blocks, dim):
    dims = list(blocks.shape[1:])
    dims[dim] *= blocks.shape[0]
    return jnp.moveaxis(blocks, 0, dim).reshape(dims)


def all_blocks(value, axes, turns):
    blocks = value[None]
    for k in turns:
        blocks = lax.all_gather(blocks, axes[k], axis=0, tiled=True)
    block = [lax.axis_size(axes[k]) for k in reversed(turns)]
    blocks = blocks.reshape(*block, *value.shape)
    turned = sorted(range(len(turns)), key=lambda place: turns[len(turns) - 1 - place])
    return blocks.transpose(*turned, *range(len(turns), blocks.ndim)).reshape(-1, *value.shape)


def whole_of(value, axes, turns, dim):
    return laid_out(all_blocks(value, axes, turns), dim)


def rms_norm(features, scale_gain):
    return (
        features
        * lax.rsqrt(jnp.mean(features * features, axis=-1, keepdims=True) + 1e-06)
        * scale_gain.astype(jnp.float32)
    )


def blocked(running, arrays, first_row, handler):
    total_rows = arrays[0].shape[0]
    block_rows = 1
    for candidate in range(min(total_rows, 1024), 0, -1):
        if total_rows % candidate == 0:
            block_rows = candidate
            break
    if block_rows == total_rows:
        return handler(running, first_row, *arrays)
    block_count = total_rows // block_rows

    def step_block(block_index, state_now):
        block_begin = block_index * block_rows
        sliced_items = tuple(
            (lax.dynamic_slice_in_dim(item, block_begin, block_rows, 0) for item in arrays)
        )
        return handler(state_now, first_row + block_begin, *sliced_items)

    return lax.fori_loop(0, block_count, step_block, running)


def body(
    node_feats,
    norm_gain,
    w_query,
    w_key,
    w_value,
    w_out,
    msg_src_w,
    msg_dst_w,
    msg_bias,
    msg_out_w,
    msg_out_bias,
    mlp_gain,
    mlp_up,
    mlp_down,
    send_list,
    send_count,
    edge_src,
    edge_dst,
    edge_count,
):
    node_rows, model_width = node_feats.shape
    head_count = HEADS
    head_size = model_width // head_count
    slot_depth = send_list.shape[2]
    normed = rms_norm(node_feats, norm_gain).astype(jnp.bfloat16)
    queries = (
        jnp.dot(normed, w_query, preferred_element_type=jnp.float32)
        .astype(jnp.bfloat16)
        .reshape(node_rows, head_count, head_size)
    )

    def attend_block(running, key_block, value_block):
        run_max, run_total, weighted_sum = running
        block_rows = key_block.shape[0]
        key_heads = key_block.reshape(block_rows, head_count, head_size)
        value_heads = value_block.reshape(block_rows, head_count, head_size)
        scores = jnp.einsum(
            "qhd,khd->hqk", queries, key_heads, preferred_element_type=jnp.float32
        ) * head_size ** (-0.5)
        new_max = jnp.maximum(run_max, jnp.max(scores, axis=-1))
        rescale = jnp.exp(run_max - new_max)
        weights = jnp.exp(scores - new_max[:, :, None])
        new_total = run_total * rescale + jnp.sum(weights, axis=-1)
        mixed = jnp.einsum(
            "hqk,khd->qhd",
            weights.astype(jnp.bfloat16),
            value_heads,
            preferred_element_type=jnp.float32,
        ).reshape(node_rows, model_width)
        column_scale = jnp.repeat(jnp.transpose(rescale), head_size, axis=1)
        return (new_max, new_total, weighted_sum * column_scale + mixed)

    def project_block(running, row_block):
        key_block = jnp.dot(row_block, w_key, preferred_element_type=jnp.float32).astype(
            jnp.bfloat16
        )
        value_block = jnp.dot(row_block, w_value, preferred_element_type=jnp.float32).astype(
            jnp.bfloat16
        )
        return attend_block(running, key_block, value_block)

    initial = (
        jnp.full((head_count, node_rows), -1e30, jnp.float32),
        jnp.zeros((head_count, node_rows), jnp.float32),
        jnp.zeros((node_rows, model_width), jnp.float32),
    )
    lists_in = lax.all_to_all(send_list[0], DOM, split_axis=0, concat_axis=0, tiled=True)
    sender_ids = jnp.arange(lists_in.shape[0], dtype=jnp.int32)
    wanted = (sender_ids[:, None] * node_rows + lists_in).reshape(-1).astype(jnp.int32)
    picked_empty = jnp.zeros((wanted.shape[0], model_width), jnp.bfloat16)

    def project_pick(running, block_start, row_block):
        attention_state, picked = running
        attention_state = project_block(attention_state, row_block)
        block_rows = row_block.shape[0]
        offset = wanted - block_start
        inside = (offset >= 0) & (offset < block_rows)
        taken_rows = row_block[jnp.clip(offset, 0, block_rows - 1)]
        picked = jnp.where(inside[:, None], taken_rows, picked)
        return (attention_state, picked)

    final_state, received_flat = blocked(
        (initial, picked_empty),
        (jax.tree.map(lambda part: whole_of(part, DOM, (0, 1, 2), 0), normed),),
        jnp.int32(0),
        project_pick,
    )
    final_total = jnp.repeat(jnp.transpose(final_state[1]), head_size, axis=1)
    attended = (final_state[2] / final_total).astype(jnp.bfloat16)
    global_part = jnp.dot(attended, w_out, preferred_element_type=jnp.float32)
    source_table = jnp.concatenate([normed, received_flat], axis=0)
    slot_total = source_table.shape[0]
    remote_live = (jnp.arange(slot_depth, dtype=jnp.int32)[None, :] < send_count[:, 0:1]).reshape(
        -1
    )
    slot_valid = jnp.concatenate(
        [jnp.ones((node_rows,), jnp.bfloat16), remote_live.astype(jnp.bfloat16)]
    )
    slot_ids = jnp.arange(slot_total, dtype=jnp.int32)
    node_ids = jnp.arange(node_rows, dtype=jnp.int32)
    lane_ids = jnp.arange(edge_src.shape[2], dtype=jnp.int32)
    edge_limit = edge_count[0]
    bias_first = msg_bias.astype(jnp.float32)
    bias_second = msg_out_bias.astype(jnp.float32)

    def tile_step(tile_index, aggregate):
        src_tile = lax.dynamic_index_in_dim(edge_src[0], tile_index, 0, keepdims=False)
        dst_tile = lax.dynamic_index_in_dim(edge_dst[0], tile_index, 0, keepdims=False)
        pick_src = (src_tile[:, None] == slot_ids[None, :]).astype(jnp.bfloat16)
        src_feats = jnp.dot(pick_src, source_table, preferred_element_type=jnp.float32).astype(
            jnp.bfloat16
        )
        in_range = (tile_index * edge_src.shape[2] + lane_ids < edge_limit).astype(jnp.float32)
        edge_live = jnp.dot(pick_src, slot_valid, preferred_element_type=jnp.float32) * in_range
        pick_dst = (dst_tile[:, None] == node_ids[None, :]).astype(jnp.bfloat16)
        dst_feats = jnp.dot(pick_dst, normed, preferred_element_type=jnp.float32).astype(
            jnp.bfloat16
        )
        pre_act = (
            jnp.dot(src_feats, msg_src_w, preferred_element_type=jnp.float32)
            + jnp.dot(dst_feats, msg_dst_w, preferred_element_type=jnp.float32)
            + bias_first
        )
        hidden = jax.nn.silu(pre_act).astype(jnp.bfloat16)
        message = (
            jnp.dot(hidden, msg_out_w, preferred_element_type=jnp.float32) + bias_second
        ).astype(jnp.bfloat16)
        spread = (pick_dst.astype(jnp.float32) * edge_live[:, None]).astype(jnp.bfloat16)
        return aggregate + lax.dot_general(
            spread, message, (((0,), (0,)), ((), ())), preferred_element_type=jnp.float32
        )

    tile_count = edge_src.shape[1]
    local_part = lax.fori_loop(
        0, tile_count, tile_step, jnp.zeros((node_rows, model_width), jnp.float32)
    )
    mid = node_feats + local_part + global_part
    mid_normed = rms_norm(mid, mlp_gain).astype(jnp.bfloat16)
    lifted = jax.nn.gelu(jnp.dot(mid_normed, mlp_up, preferred_element_type=jnp.float32)).astype(
        jnp.bfloat16
    )
    return mid + jnp.dot(lifted, mlp_down, preferred_element_type=jnp.float32)


def solution(mesh):
    finer = Mesh(
        mesh.devices.reshape(mesh.shape["graphs"], 4, 8, 2), ("graphs", "dom_0", "dom_1", "dom_2")
    )
    placed = (
        P(GRAPHS_DOM, None),
        P(),
        P(),
        P(),
        P(),
        P(),
        P(),
        P(),
        P(),
        P(),
        P(),
        P(),
        P(),
        P(),
        P(GRAPHS_DOM, None, None),
        P("graphs", DOM),
        P(GRAPHS_DOM, None, None),
        P(GRAPHS_DOM, None, None),
        P(GRAPHS_DOM),
    )
    return jax.shard_map(
        body, mesh=finer, in_specs=placed, out_specs=P(GRAPHS_DOM, None), check_vma=False
    )
```

profile of v0, /device:TPU:1, one launch (start us, length us, event | category | flops | bytes accessed | tf_op | source)
XLA Modules:
  0.0 176.1 jit_solution(1076968867520439703)
XLA Ops:
  6.5 1.1 multiply_reduce_fusion.1
  7.6 1.0 multiply_convert_fusion.4
  8.6 13.4 %all-gather = bf16[512,256]{1,0:T(8,128)(2,1)} all-gather(bf16[128,256]{1,0:T(8,128)(2,1)S(1)} %multiply_convert_fusion.4), channel_id=2, replica_groups=mesh['graphs'=8,'dom_0'=4,'dom_1'=8,'dom_2'=2] {'dom_0'}, dimensions={0}, use_global_device_ids=true | all-gather | bytes 327680 | tf_op jit(solution)/shard_map/all_gather | solution.py:21
  22.1 47.2 %all-gather.4.cloned.1.call-done = bf16[32,128,256]{2,1,0:T(8,128)(2,1)} async-done(((bf16[4,128,256]{2,1,0:T(8,128)(2,1)}), bf16[32,128,256]{2,1,0:T(8,128)(2,1)}) %all-gather.4.cloned.1.call-update) | async-done | bytes 2097168 | tf_op jit(solution)/shard_map/all_gather | solution.py:21
  69.3 1.4 copy.30
  70.6 12.4 %all-to-all-start = ((s32[64,1,4]{2,1,0:T(1,128)}), s32[64,1,4]{2,1,0:T(1,128)S(1)}, u32[]{:S(2)}, u32[]{:S(2)}) async-start(s32[64,1,4]{2,1,0:T(1,128)} %bitcast.7), calls=%async_computation | async-start | bytes 65536 | tf_op jit(solution)/shard_map/all_to_all | solution.py:128
  83.1 0.7 iota_compare_fusion.7
  83.9 1.1 convolution_convert_fusion.4
  85.4 7.3 %all-to-all-done = s32[64,1,4]{2,1,0:T(1,128)S(1)} async-done(((s32[64,1,4]{2,1,0:T(1,128)}), s32[64,1,4]{2,1,0:T(1,128)S(1)}, u32[]{:S(2)}, u32[]{:S(2)}) %all-to-all-start) | async-done | bytes 1056 | tf_op jit(solution)/shard_map/all_to_all | solution.py:128
  93.1 0.7 reduce.3
  94.0 3.0 %all-gather.6.cloned.1.call-done = bf16[64,128,256]{2,1,0:T(8,128)(2,1)} async-done(((bf16[32,128,256]{2,1,0:T(8,128)(2,1)}), bf16[64,128,256]{2,1,0:T(8,128)(2,1)}) %all-gather.6.cloned.1.call-update) | async-done | bytes 4194320 | tf_op jit(solution)/shard_map/all_gather | solution.py:21
  97.0 4.7 %copy.28 = bf16[4,8,2,128,256]{4,3,2,1,0:T(8,128)(2,1)} copy(bf16[4,8,2,128,256]{4,3,0,1,2:T(8,128)(2,1)} %bitcast.121) | data formatting | bytes 8388608 | tf_op jit(solution)/shard_map/transpose | solution.py:25
  101.7 44.4 %while.36 = (s32[]{:T(128)}, f32[8,128]{1,0:T(8,128)S(1)}, f32[8,128]{1,0:T(8,128)S(1)}, f32[128,256]{0,1:T(8,128)S(1)}, bf16[256,256]{1,0:T(8,128)(2,1)S(1)}, /...) while((s32[]{:T(128)}, f32[8,128]{1,0:T(8,128)S(1)}, ...), condition=%wide.region_4.5_spmd.clone, body=%wide.region_1.4_spmd.clone.sunk | while | flops 411804928 | bytes 18362064 | solution.py:58
  101.8 1.2 constant_dynamic-slice_fusion.2
  103.0 1.2 gather_fusion
  104.9 0.8 bitcast_reduce_fusion.2
  105.8 0.8 fusion.101
  106.6 0.7 fusion.99
  107.4 1.1 constant_dynamic-slice_fusion.2
  108.5 1.2 gather_fusion
  110.5 0.8 bitcast_reduce_fusion.2
  111.3 0.8 fusion.101
  113.0 1.1 constant_dynamic-slice_fusion.2
  114.0 1.2 gather_fusion
  116.0 0.8 bitcast_reduce_fusion.2
  116.9 0.8 fusion.101
  118.5 1.1 constant_dynamic-slice_fusion.2
  119.6 1.2 gather_fusion
  121.6 0.8 bitcast_reduce_fusion.2
  122.4 0.8 fusion.101
  124.0 1.1 constant_dynamic-slice_fusion.2
  125.1 1.2 gather_fusion
  127.1 0.8 bitcast_reduce_fusion.2
  127.9 0.8 fusion.101
  129.6 1.1 constant_dynamic-slice_fusion.2
  130.7 1.2 gather_fusion
  132.6 0.8 bitcast_reduce_fusion.2
  133.5 0.8 fusion.101
  135.1 1.1 constant_dynamic-slice_fusion.2
  136.2 1.2 gather_fusion
  138.2 0.8 bitcast_reduce_fusion.2
  139.0 0.8 fusion.101
  140.7 1.1 constant_dynamic-slice_fusion.2
  141.7 1.2 gather_fusion
  143.7 0.8 bitcast_reduce_fusion.2
  144.6 0.8 fusion.101
  146.3 21.5 %while.37 = (s32[]{:T(128)}, f32[128,256]{1,0:T(8,128)S(1)}, s32[1,8,128]{2,1,0:T(8,128)}, s32[]{:T(128)}, s32[1,8,128]{2,1,0:T(8,128)}, /*index=5*/bf16[384]{0:...) while((s32[]{:T(128)}, f32[128,256]{1,0:T(8,128)S(1)}, ...), condition=%wide.region_6.7_spmd.clone.clone, body=%wide.region_5.6_spmd.clone.clone.sunk | while | flops 92995968 | bytes 1320383 | solution.py:195
  146.3 0.8 dynamic-slice_bitcast_fusion.3
  147.1 0.9 fusion.110
  149.0 0.7 dynamic-slice_bitcast_fusion.3
  149.7 0.9 fusion.110
  151.7 0.7 dynamic-slice_bitcast_fusion.3
  152.4 0.9 fusion.110
  154.4 0.7 dynamic-slice_bitcast_fusion.3
  155.1 0.9 fusion.110
  157.0 0.7 dynamic-slice_bitcast_fusion.3
  157.8 0.9 fusion.110
  159.7 0.7 dynamic-slice_bitcast_fusion.3
  160.4 0.9 fusion.110
  162.4 0.7 dynamic-slice_bitcast_fusion.3
  163.1 0.9 fusion.110
  165.1 0.7 dynamic-slice_bitcast_fusion.3
  165.8 0.9 fusion.110
  168.1 1.1 convolution_add_fusion.3
  (174 shorter events, 22.0 us)
Async XLA Ops:
  6.5 161.6 %copy-start = (bf16[1024,256]{1,0:T(8,128)(2,1)S(1)}, bf16[1024,256]{1,0:T(8,128)(2,1)}, u32[]{:S(2)}) copy-start(bf16[1024,256]{1,0:T(8,128)(2,1)} %param.36) | copy-start | bytes 1572868
  6.5 62.7 %all-gather.4.cloned.1.call-start = ((), (), s32[]{:S(2)}) async-start(), calls=%async_computation.1 | async-start | bytes 2359296 | tf_op jit(solution)/shard_map/all_gather | solution.py:21
  22.0 75.0 %all-gather.6.cloned.1.call-start = ((), (), s32[]{:S(2)}) async-start(), calls=%async_computation.2 | async-start | bytes 6291456 | tf_op jit(solution)/shard_map/all_gather | solution.py:21
  70.6 22.0 %all-to-all-start = ((s32[64,1,4]{2,1,0:T(1,128)}), s32[64,1,4]{2,1,0:T(1,128)S(1)}, u32[]{:S(2)}, u32[]{:S(2)}) async-start(s32[64,1,4]{2,1,0:T(1,128)} %bitcast.7), calls=%async_computation | async-start | bytes 65536 | tf_op jit(solution)/shard_map/all_to_all | solution.py:128
  97.0 4.7 %copy-start.1 = (bf16[256,256]{1,0:T(8,128)(2,1)S(1)}, bf16[256,256]{1,0:T(8,128)(2,1)}, u32[]{:S(2)}) copy-start(bf16[256,256]{1,0:T(8,128)(2,1)} %param.26) | copy-start | bytes 393220
  97.0 4.7 %copy-start.2 = (bf16[256,256]{1,0:T(8,128)(2,1)S(1)}, bf16[256,256]{1,0:T(8,128)(2,1)}, u32[]{:S(2)}) copy-start(bf16[256,256]{1,0:T(8,128)(2,1)} %param.27) | copy-start | bytes 393220
  101.7 44.5 %copy-start.3 = (bf16[256,256]{1,0:T(8,128)(2,1)S(1)}, bf16[256,256]{1,0:T(8,128)(2,1)}, u32[]{:S(2)}) copy-start(bf16[256,256]{1,0:T(8,128)(2,1)} %param.29) | copy-start | bytes 393220
  101.7 44.5 %copy-start.4 = (bf16[256,256]{1,0:T(8,128)(2,1)S(1)}, bf16[256,256]{1,0:T(8,128)(2,1)}, u32[]{:S(2)}) copy-start(bf16[256,256]{1,0:T(8,128)(2,1)} %param.32) | copy-start | bytes 393220
  101.7 44.5 %copy-start.7 = (f32[256]{0:T(256)S(1)}, f32[256]{0:T(256)}, u32[]{:S(2)}) copy-start(f32[256]{0:T(256)} %param.33) | copy-start | bytes 3076
  101.7 44.5 %copy-start.9 = (bf16[256,256]{1,0:T(8,128)(2,1)S(1)}, bf16[256,256]{1,0:T(8,128)(2,1)}, u32[]{:S(2)}) copy-start(bf16[256,256]{1,0:T(8,128)(2,1)} %param.30) | copy-start | bytes 393220
  101.7 44.5 %copy-start.10 = (f32[256]{0:T(256)S(1)}, f32[256]{0:T(256)}, u32[]{:S(2)}) copy-start(f32[256]{0:T(256)} %param.31) | copy-start | bytes 3076
  146.2 21.6 %copy-start.5 = (f32[128,256]{1,0:T(8,128)S(1)}, f32[128,256]{1,0:T(8,128)}, u32[]{:S(2)}) copy-start(f32[128,256]{1,0:T(8,128)} %param.23) | copy-start | bytes 393220
  146.2 21.6 %copy-start.6 = (bf16[256,256]{1,0:T(8,128)(2,1)S(1)}, bf16[256,256]{1,0:T(8,128)(2,1)}, u32[]{:S(2)}) copy-start(bf16[256,256]{1,0:T(8,128)(2,1)} %param.28) | copy-start | bytes 393220
  146.2 21.9 %copy-start.8 = (bf16[256,1024]{1,0:T(8,128)(2,1)S(1)}, bf16[256,1024]{1,0:T(8,128)(2,1)}, u32[]{:S(2)}) copy-start(bf16[256,1024]{1,0:T(8,128)(2,1)} %param.35) | copy-start | bytes 1572868
  146.2 21.9 %copy-start.11 = (f32[256]{0:T(256)S(1)}, f32[256]{0:T(256)}, u32[]{:S(2)}) copy-start(f32[256]{0:T(256)} %param.34) | copy-start | bytes 3076
Sparse Core Ops, SparseCore 0:
  22.1 47.0 all-gather.3
  71.3 25.6 all-gather.5
where the time goes:
time: 177 us; the launch traced here: 176 us
  waiting for transfers between devices  57.4 us (32%)
  matrix products  36.3 us (21%)
  local copies, waits for them, and re-layouts  31 us (18%)
  between operations  13.7 us (8%)
  blocking collectives  13.4 us (8%)
  starting transfers between devices  12.5 us (7%)
  other arithmetic  10.7 us (6%)
    all_gather x2, waiting for transfers between devices, all_blocks(): blocks = lax.all_gather(blocks, axes[k], axis=0, tiled=True)  50.1 us
    all_gather x1, blocking collectives, all_blocks(): blocks = lax.all_gather(blocks, axes[k], axis=0, tiled=True)  13.4 us
    all_to_all x1, starting transfers between devices, body(): lax.all_to_all(send_list[0], DOM, split_axis=0, concat_axis=0, tiled=True)  12.4 us
    gather x8, local copies, waits for them, and re-layouts, project_pick(): taken_rows = row_block[jnp.clip(offset, 0, block_rows - 1)]  9.22 us
    dynamic_slice x8, local copies, waits for them, and re-layouts, step_block(): lax.dynamic_slice_in_dim(item, block_begin, block_rows, 0)  8.76 us
    all_to_all x1, waiting for transfers between devices, body(): lax.all_to_all(send_list[0], DOM, split_axis=0, concat_axis=0, tiled=True)  7.26 us
    dot_general x8, matrix products, tile_step(): jnp.dot(pick_src, slot_valid, preferred_element_type=jnp.float32) * in_range  6.85 us
    dot_general x8, matrix products, attend_block(): jnp.einsum('qhd,khd->hqk', queries, key_heads, preferred_element_type=jnp...  6.63 us
  transfers between devices with their start and end apart: 3, of which 3 were waited for; matrix products, arithmetic and copies ran while one was open for 3% of the time, Pallas kernels for 0%

commit v1 on v0

v1 whole, which is shorter than its diff:
```python
import functools
import math

import jax
import jax.numpy as jnp
from jax import lax
from jax.experimental import pallas as pl
from jax.experimental.pallas import tpu as pltpu
from jax.sharding import Mesh
from jax.sharding import PartitionSpec as P

HEADS = 8
NODES = 128
WIDTH = 256
HEAD = WIDTH // HEADS
SLOTS = 4
DOMS = 64
DOM = ("ya", "yb", "za", "zb", "core")
GRAPHS_DOM = ("graphs",) + DOM
HEAD_AXES = ("ya", "za")
CHIP_AXES = ("yb", "zb")
CHIPS = 4
F32 = jnp.float32
BF16 = jnp.bfloat16
SCALE = math.log2(math.e) / math.sqrt(HEAD)
VM = pl.BlockSpec(memory_space=pltpu.VMEM)
SM = pl.BlockSpec(memory_space=pltpu.SMEM)
KV_ROWS = 8 * 2 * HEAD
SENT_ROWS = KV_ROWS + 8 * 16


def iota(shape, dim):
    return lax.broadcasted_iota(jnp.int32, shape, dim)


def mm(a, b, dims=((1,), (0,))):
    return lax.dot_general(a, b, (dims, ((), ())), preferred_element_type=F32)


def rms(x, gain):
    return x * lax.rsqrt(jnp.mean(x * x, axis=-1, keepdims=True) + 1e-06) * gain


def project_kernel(feats, gain, wq, wk, wv, lists, normed_out, sent):
    normed = rms(feats[...], gain[...]).astype(BF16)
    normed_out[...] = normed
    for first, weight, factor in ((0, wq, SCALE), (HEAD, wk, None), (2 * HEAD, wv, None)):
        out = mm(normed, weight[...])
        if factor is not None:
            out = out * factor
        turned = out.T.astype(BF16)
        for h in range(HEADS):
            sent[h, first : first + HEAD, :] = turned[h * HEAD : (h + 1) * HEAD, :]
    place = iota((DOMS * SLOTS, DOMS), 0)
    receiver = (
        ((place >> 7) & 1) * 32
        + ((place >> 4) & 1) * 16
        + ((place >> 5) & 3) * 4
        + ((place >> 2) & 3)
    )
    pick_receiver = (receiver == iota((DOMS * SLOTS, DOMS), 1)).astype(BF16)
    spread = mm(pick_receiver, lists[0].astype(F32).astype(BF16), ((1,), (1,)))
    own_slot = (iota(spread.shape, 0) & 3) == iota(spread.shape, 1)
    index = jnp.sum(jnp.where(own_slot, spread, 0.0), axis=1, keepdims=True)
    lanes = iota((DOMS * SLOTS, NODES), 1).astype(F32)
    rows = mm((lanes == index).astype(BF16), normed)
    for h in range(HEADS):
        parts = []
        for chip in range(CHIPS):
            at = h * 32 + chip * 8
            parts += [rows[at : at + 8, :128], rows[at : at + 8, 128:]]
        sent[h, 3 * HEAD :, :] = jnp.concatenate(parts, axis=0).astype(BF16)


def repack_kernel(got, sent):
    for chip in range(CHIPS):
        for s in range(8):
            sent[chip, s * 64 : (s + 1) * 64, :] = got[s, HEAD : 3 * HEAD, :]
            sent[chip, KV_ROWS + s * 16 : KV_ROWS + (s + 1) * 16, :] = got[
                s, 96 + chip * 16 : 112 + chip * 16, :
            ]


KEYS = CHIPS * 8 * NODES
QUERIES = 8 * NODES
Q_BLOCK = 256


def load_operands(got, kv, q_s, k_s, v_s):
    for s in range(8):
        q_s[s * 128 : (s + 1) * 128, :] = got[s, 0:HEAD, :].T
    for chip in range(CHIPS):
        for s in range(8):
            at = (chip * 8 + s) * 128
            k_s[:, at : at + 128] = kv[chip, s * 64 : s * 64 + 32, :]
            v_s[0:32, at : at + 128] = kv[chip, s * 64 + 32 : s * 64 + 64, :]
    v_s[32:64, :] = jnp.ones((32, KEYS), BF16)


def attend_first_kernel(got, kv, acc_out, max_out, q_s, k_s, v_s):
    load_operands(got, kv, q_s, k_s, v_s)
    for b in range(QUERIES // Q_BLOCK):
        at = slice(b * Q_BLOCK, (b + 1) * Q_BLOCK)
        scores = mm(q_s[at, :], k_s[...])
        top = jnp.max(scores, axis=1, keepdims=True)
        weights = jnp.exp2(scores - top).astype(BF16)
        acc_out[at, :] = mm(weights, v_s[...], ((1,), (1,)))
        max_out[at, :] = jnp.broadcast_to(top, (Q_BLOCK, 128))


def attend_last_kernel(got, kv, acc_in, max_in, out, q_s, k_s, v_s):
    load_operands(got, kv, q_s, k_s, v_s)
    for b in range(QUERIES // Q_BLOCK):
        at = slice(b * Q_BLOCK, (b + 1) * Q_BLOCK)
        scores = mm(q_s[at, :], k_s[...])
        before = max_in[at, 0:1]
        top = jnp.maximum(before, jnp.max(scores, axis=1, keepdims=True))
        weights = jnp.exp2(scores - top).astype(BF16)
        acc = acc_in[at, :] * jnp.exp2(before - top) + mm(weights, v_s[...], ((1,), (1,)))
        done = (acc[:, 0:32] / acc[:, 32:33]).T.astype(BF16)
        for i in range(Q_BLOCK // 128):
            out[b * (Q_BLOCK // 128) + i] = done[:, i * 128 : (i + 1) * 128]


def edge_kernel(
    limit, place, normed, mine, other, counts, src, dst, w_src, w_dst, b1, w_out, b2, feats, out
):
    edges = src.shape[1] * src.shape[2]
    tiles = src.shape[1]
    row = lambda ref: jnp.concatenate([ref[0, t : t + 1, :] for t in range(tiles)], axis=1)
    src_row, dst_row = row(src), row(dst)
    core = place[0]
    table = [normed[...].astype(F32)]
    for part in (mine, other):
        for chip in range(CHIPS):
            for s in range(8):
                pair = part[chip, KV_ROWS + s * 16 : KV_ROWS + (s + 1) * 16, :].astype(F32)
                table.append(jnp.concatenate([pair[:8], pair[8:]], axis=1))
    table = jnp.concatenate(table, axis=0).astype(BF16)
    total = 512
    at = iota((total, 1), 0)
    sender_core = jnp.where(at >= 256, 1 - core, core)
    chip, s, to, slot = (at >> 6) & 3, (at >> 3) & 7, (at >> 2) & 1, at & 3
    sender = (
        (s >> 2) * 32 + (chip >> 1) * 16 + (s & 3) * 4 + (chip & 1) * 2 + sender_core
    )
    wide = iota((total, DOMS), 1)
    held = jnp.broadcast_to(counts[...].astype(F32), (8, DOMS)).astype(BF16)
    count = mm((sender == wide).astype(BF16), held, ((1,), (1,)))[:, 0:1]
    live_slot = (to == core) & (slot.astype(F32) < count)
    ids = jnp.where(live_slot, NODES + sender * SLOTS + slot, -1)
    ids = jnp.concatenate([iota((NODES, 1), 0), ids], axis=0)
    pick = (ids == src_row).astype(F32).astype(BF16)
    to_node = iota((NODES, 1), 0) == dst_row
    pick_dst = to_node.astype(F32).astype(BF16)
    hit = mm(jnp.ones((8, ids.shape[0]), BF16), pick)[0:1, :]
    live = jnp.where(iota((1, edges), 1) < limit[0], hit, 0.0)
    src_feats = mm(table, pick, ((0,), (0,))).astype(BF16)
    dst_feats = mm(normed[...], pick_dst, ((0,), (0,))).astype(BF16)
    column = lambda ref: jnp.broadcast_to(ref[...], (8, WIDTH)).T[:, 0:1]
    pre = (
        mm(w_src[...], src_feats, ((0,), (0,)))
        + mm(w_dst[...], dst_feats, ((0,), (0,)))
        + column(b1)
    )
    hidden = jax.nn.silu(pre).astype(BF16)
    message = (mm(w_out[...], hidden, ((0,), (0,))) + column(b2)).astype(BF16)
    spread = jnp.where(to_node, live, 0.0).astype(BF16)
    out[...] = feats[...] + mm(spread, message, ((1,), (1,)))


def finish_kernel(base, attended, w_out, gain, up, down, out):
    turned = jnp.concatenate([attended[h] for h in range(HEADS)], axis=0)
    mid = base[...] + mm(turned, w_out[...], ((0,), (0,)))
    lifted = jax.nn.gelu(mm(rms(mid, gain[...]).astype(BF16), up[...])).astype(BF16)
    out[...] = mid + mm(lifted, down[...])


def body(
    node_feats,
    norm_gain,
    w_query,
    w_key,
    w_value,
    w_out,
    msg_src_w,
    msg_dst_w,
    msg_bias,
    msg_out_w,
    msg_out_bias,
    mlp_gain,
    mlp_up,
    mlp_down,
    send_list,
    send_count,
    edge_src,
    edge_dst,
    edge_count,
):
    shape = jax.ShapeDtypeStruct
    row = lambda v: v.reshape(1, WIDTH)
    normed, sent = pl.pallas_call(
        project_kernel,
        out_shape=(shape((NODES, WIDTH), BF16), shape((HEADS, 160, 128), BF16)),
        in_specs=[VM] * 6,
        out_specs=(VM, VM),
        name="project",
    )(node_feats, row(norm_gain), w_query, w_key, w_value, jnp.swapaxes(send_list, 1, 2))
    got = lax.all_to_all(sent, HEAD_AXES, 0, 0, tiled=True)
    shared = pl.pallas_call(
        repack_kernel,
        out_shape=shape((CHIPS, SENT_ROWS, 128), BF16),
        in_specs=[VM],
        out_specs=VM,
        name="repack",
    )(got)
    mine = lax.all_to_all(shared, CHIP_AXES, 0, 0, tiled=True)
    other = lax.ppermute(mine, "core", [(0, 1), (1, 0)])
    scratch = [
        pltpu.VMEM((QUERIES, HEAD), BF16),
        pltpu.VMEM((HEAD, KEYS), BF16),
        pltpu.VMEM((2 * HEAD, KEYS), BF16),
    ]
    acc, top = pl.pallas_call(
        attend_first_kernel,
        out_shape=(shape((QUERIES, 64), F32), shape((QUERIES, 128), F32)),
        in_specs=[VM] * 2,
        out_specs=(VM, VM),
        scratch_shapes=scratch,
        name="attend_first",
    )(got, mine)
    attended = pl.pallas_call(
        attend_last_kernel,
        out_shape=shape((8, HEAD, NODES), BF16),
        in_specs=[VM] * 4,
        out_specs=VM,
        scratch_shapes=scratch,
        name="attend_last",
    )(got, other, acc, top)
    back = lax.all_to_all(attended, HEAD_AXES, 0, 0, tiled=True)
    core = lax.axis_index("core").reshape(1).astype(jnp.int32)
    base = pl.pallas_call(
        edge_kernel,
        out_shape=shape((NODES, WIDTH), F32),
        in_specs=[SM, SM] + [VM] * 12,
        out_specs=VM,
        name="edges",
    )(
        edge_count,
        core,
        normed,
        mine,
        other,
        send_count.T,
        edge_src,
        edge_dst,
        msg_src_w,
        msg_dst_w,
        row(msg_bias),
        msg_out_w,
        row(msg_out_bias),
        node_feats,
    )
    return pl.pallas_call(
        finish_kernel,
        out_shape=shape((NODES, WIDTH), F32),
        in_specs=[VM] * 6,
        out_specs=VM,
        name="finish",
    )(base, back, w_out, row(mlp_gain), mlp_up, mlp_down)


def solution(mesh):
    finer = Mesh(
        mesh.devices.reshape(mesh.shape["graphs"], 2, 2, 4, 2, 2), ("graphs",) + DOM
    )
    rows = P(GRAPHS_DOM, None)
    blocks = P(GRAPHS_DOM, None, None)
    placed = (rows,) + (P(),) * 13 + (blocks, P("graphs", DOM), blocks, blocks, P(GRAPHS_DOM))
    return jax.shard_map(body, mesh=finer, in_specs=placed, out_specs=rows, check_vma=False)
```

time: 177 us -> 80.7 us (0.46)
  waiting for transfers between devices: 57.4 us -> 3.67 us
  matrix products: 36.3 us -> 0 us
  local copies, waits for them, and re-layouts: 31 us -> 1.46 us
  Pallas kernels: 0 us -> 27.4 us
  blocking collectives: 13.4 us -> 38 us
  between operations: 13.7 us -> 0.68 us
  other arithmetic: 10.7 us -> 0 us
  starting transfers between devices: 12.5 us -> 8.75 us
    all_gather x2 -> x0, waiting for transfers between devices: 50.1 us -> none  [all_blocks(): blocks = lax.all_gather(blocks, axes[k], axis=0, tiled=True)]
    all_to_all x0 -> x2, blocking collectives: none -> 38 us  [the longest x1 27.1 us: body(): got = lax.all_to_all(sent, HEAD_AXES, 0, 0, tiled=True)]
    dot_general x67 -> x0, matrix products: 36.3 us -> none  [the longest x8 6.85 us: tile_step(): jnp.dot(pick_src, slot_valid, preferred_element_type=jnp.float32) * in_range]
    pallas_call x0 -> x6, Pallas kernels: none -> 27.4 us  [the longest x1 8.18 us: body(): pl.pallas_call(attend_last_kernel, out_shape=shape((8, HEAD, NODES), BF16...]
    all_gather x1 -> x0, blocking collectives: 13.4 us -> none  [all_blocks(): blocks = lax.all_gather(blocks, axes[k], axis=0, tiled=True)]
    gather x8 -> x0, local copies, waits for them, and re-layouts: 9.22 us -> none  [project_pick(): taken_rows = row_block[jnp.clip(offset, 0, block_rows - 1)]]
    all_to_all x1, starting transfers between devices: 12.4 us -> 3.35 us  [body(): back = lax.all_to_all(attended, HEAD_AXES, 0, 0, tiled=True)]
    dynamic_slice x8 -> x0, local copies, waits for them, and re-layouts: 8.76 us -> none  [step_block(): lax.dynamic_slice_in_dim(item, block_begin, block_rows, 0)]
  transfers between devices with their start and end apart: 3 -> 2, of which waited for: 3 -> 1; matrix products, arithmetic and copies ran while one was open for 3% -> 0% of each run, Pallas kernels for 0% -> 15%
where the time goes in v1:
time: 80.7 us; the launch traced here: 79.9 us
  blocking collectives  38 us (47%)
  Pallas kernels  27.4 us (34%)
  starting transfers between devices  8.75 us (11%)
  waiting for transfers between devices  3.67 us (5%)
  local copies, waits for them, and re-layouts  1.46 us (2%)
    all_to_all x1, blocking collectives, body(): got = lax.all_to_all(sent, HEAD_AXES, 0, 0, tiled=True)  27.1 us
    all_to_all x1, blocking collectives, body(): mine = lax.all_to_all(shared, CHIP_AXES, 0, 0, tiled=True)  10.8 us
    pallas_call x1, Pallas kernels, body(): pl.pallas_call(attend_last_kernel, out_shape=shape((8, HEAD, NODES), BF16...  8.18 us
    pallas_call x1, Pallas kernels, body(): pl.pallas_call(attend_first_kernel, out_shape=(shape((QUERIES, 64), F32),...  8.03 us
    ppermute x1, starting transfers between devices, body(): other = lax.ppermute(mine, 'core', [(0, 1), (1, 0)])  5.4 us
    pallas_call x1, Pallas kernels, body(): pl.pallas_call(edge_kernel, out_shape=shape((NODES, WIDTH), F32), in_spec...  4.17 us
    all_to_all x1, waiting for transfers between devices, body(): back = lax.all_to_all(attended, HEAD_AXES, 0, 0, tiled=True)  3.66 us
    all_to_all x1, starting transfers between devices, body(): back = lax.all_to_all(attended, HEAD_AXES, 0, 0, tiled=True)  3.35 us
  transfers between devices with their start and end apart: 2, of which 1 were waited for; matrix products, arithmetic and copies ran while one was open for 0% of the time, Pallas kernels for 15%

profile of v1, /device:TPU:1, one launch (start us, length us, event | category | flops | bytes accessed | tf_op | source)
XLA Modules:
  0.0 79.9 jit_solution(12242950564504456896)
XLA Ops:
  0.0 2.4 %project.1 = (bf16[128,256]{1,0:T(8,128)(2,1)}, bf16[8,160,128]{2,1,0:T(8,128)(2,1)}) custom-call(f32[128,256]{1,0:T(8,128)} %feats.3, f32[1,256]{1,0:T(1,128)} %bitcast.10, bf16[256,256]{1,0:T(8,128)(2,1)} %wq.1, bf16[256,256]{1,0:T(8,128)(2,1)} %wk.1, bf16[256,256]{1,0:T(8,128)(2,1)} %wv.1, s32[1,4,64]{2,1,0:T(4,128)} %bitcast.7), custom_call_target="tpu_custom_call" | custom-call | tf_op jit(solution)/shard_map/project/pallas_call | solution.py:202
  2.4 27.1 %all_to_all.15.got = bf16[8,160,128]{2,1,0:T(8,128)(2,1)} all-to-all(bf16[8,160,128]{2,1,0:T(8,128)(2,1)} %get-tuple-element.10), channel_id=1, replica_groups=mesh['graphs'=8,'ya'=2,'yb'=2,'za'=4,'zb'=2,'core'=2] {'ya','za'}, dimensions={0} | all-to-all | bytes 655360 | tf_op jit(solution)/shard_map/all_to_all | solution.py:209
  29.5 1.9 %repack.1 = bf16[4,640,128]{2,1,0:T(8,128)(2,1)} custom-call(bf16[8,160,128]{2,1,0:T(8,128)(2,1)} %all_to_all.15.got), custom_call_target="tpu_custom_call" | custom-call | tf_op jit(solution)/shard_map/repack/pallas_call | solution.py:210
  31.4 10.8 %all_to_all.16.mine.kv = bf16[4,640,128]{2,1,0:T(8,128)(2,1)S(1)} all-to-all(bf16[4,640,128]{2,1,0:T(8,128)(2,1)} %repack.1), channel_id=1, replica_groups=mesh['graphs'=8,'ya'=2,'yb'=2,'za'=4,'zb'=2,'core'=2] {'yb','zb'}, dimensions={0} | all-to-all | bytes 1310720 | tf_op jit(solution)/shard_map/all_to_all | solution.py:217
  42.3 0.0 copy-start
  42.3 5.4 %collective-permute-start = (bf16[4,640,128]{2,1,0:T(8,128)(2,1)S(1)}, bf16[4,640,128]{2,1,0:T(8,128)(2,1)S(1)}, u32[]{:S(2)}, u32[]{:S(2)}) collective-permute-start(bf16[4,640,128]{2,1,0:T(8,128)(2,1)S(1)} %all_to_all.16.mine.kv), channel_id=1, source_target_pairs={{0,1},{1,0},{2,3},{3,2},{4,5},{5,4},{6,7},{7,6},{8,9},{9,8},{10,11... | collective-permute-start | bytes 1966088 | tf_op jit(solution)/shard_map/ppermute | solution.py:218
  47.7 0.0 copy-done
  47.7 8.0 %attend_first.1 = (f32[1024,64]{1,0:T(8,128)}, f32[1024,128]{1,0:T(8,128)}) custom-call(bf16[8,160,128]{2,1,0:T(8,128)(2,1)} %all_to_all.15.got, bf16[4,640,128]{2,1,0:T(8,128)(2,1)} %copy-done), custom_call_target="tpu_custom_call" | custom-call | tf_op jit(solution)/shard_map/attend_first/pallas_call | solution.py:224
  55.7 0.0 collective-permute-done.other.kv
  55.7 0.0 copy-start.1
  55.7 0.8 %copy-done.1 = bf16[4,640,128]{2,1,0:T(8,128)(2,1)} copy-done((bf16[4,640,128]{2,1,0:T(8,128)(2,1)}, bf16[4,640,128]{2,1,0:T(8,128)(2,1)S(1)}, u32[]{:S(2)}) %copy-start.1) | copy-done | bytes 655384
  56.6 8.2 %attend_last.1 = bf16[8,32,128]{2,1,0:T(8,128)(2,1)} custom-call(bf16[8,160,128]{2,1,0:T(8,128)(2,1)} %all_to_all.15.got, bf16[4,640,128]{2,1,0:T(8,128)(2,1)} %copy-done.1, f32[1024,64]{1,0:T(8,128)} %get-tuple-element.11.acc_in, f32[1024,128]{1,0:T(8,128)} %get-tuple-element.12.max_in), custom_call_target="tpu_custom_call" | custom-call | tf_op jit(solution)/shard_map/attend_last/pallas_call | solution.py:232
  64.7 3.3 %all-to-all-start.2 = ((bf16[8,32,128]{2,1,0:T(8,128)(2,1)}), bf16[8,32,128]{2,1,0:T(8,128)(2,1)S(1)}, u32[]{:S(2)}, u32[]{:S(2)}) async-start(bf16[8,32,128]{2,1,0:T(8,128)(2,1)} %attend_last.1), calls=%async_computation.2 | async-start | bytes 131072 | tf_op jit(solution)/shard_map/all_to_all | solution.py:240
  68.7 4.2 %edges.1.base = f32[128,256]{1,0:T(8,128)} custom-call(s32[1]{0:T(128)S(6)} %copy.20.limit, s32[1]{0:T(128)} %bitcast.place, bf16[128,256]{1,0:T(8,128)(2,1)} %get-tuple-element.9.normed, bf16[4,640,128]{2,1,0:T(8,128)(2,1)} %copy-done, bf16[4,640,128]{2,1,0:T(8,128)(2,1)} %copy-done.1, s32[1,64]{1,0:T(1,128)} %bitcast.12, s32[1,8,128]{2,1,0:T(8,128)} %src.1, ...), custom_call_target="tpu_custom_call" | custom-call | tf_op jit(solution)/shard_map/edges/pallas_call | solution.py:242
  72.9 3.7 %all-to-all-done.2.attended = bf16[8,32,128]{2,1,0:T(8,128)(2,1)S(1)} async-done(((bf16[8,32,128]{2,1,0:T(8,128)(2,1)}), bf16[8,32,128]{2,1,0:T(8,128)(2,1)S(1)}, u32[]{:S(2)}, u32[]{:S(2)}) %all-to-all-start.2) | async-done | bytes 65568 | tf_op jit(solution)/shard_map/all_to_all | solution.py:240
  76.6 0.0 copy-start.2
  76.6 0.6 copy-done.2
  77.2 2.7 %finish.1 = f32[128,256]{1,0:T(8,128)} custom-call(f32[128,256]{1,0:T(8,128)} %edges.1.base, bf16[8,32,128]{2,1,0:T(8,128)(2,1)} %copy-done.2, bf16[256,256]{1,0:T(8,128)(2,1)} %w_out.3, f32[1,256]{1,0:T(1,128)} %bitcast.11, bf16[256,1024]{1,0:T(8,128)(2,1)} %up.1, bf16[1024,256]{1,0:T(8,128)(2,1)} %down.1), custom_call_target="tpu_custom_call" | custom-call | tf_op jit(solution)/shard_map/finish/pallas_call | solution.py:264
Async XLA Ops:
  42.3 5.4 %copy-start = (bf16[4,640,128]{2,1,0:T(8,128)(2,1)}, bf16[4,640,128]{2,1,0:T(8,128)(2,1)S(1)}, u32[]{:S(2)}) copy-start(bf16[4,640,128]{2,1,0:T(8,128)(2,1)S(1)} %all_to_all.16.mine.kv) | copy-start | bytes 1966084
  42.3 13.5 %collective-permute-start = (bf16[4,640,128]{2,1,0:T(8,128)(2,1)S(1)}, bf16[4,640,128]{2,1,0:T(8,128)(2,1)S(1)}, u32[]{:S(2)}, u32[]{:S(2)}) collective-permute-start(bf16[4,640,128]{2,1,0:T(8,128)(2,1)S(1)} %all_to_all.16.mine.kv), channel_id=1, source_target_pairs={{0,1},{1,0},{2,3},{3,2},{4,5},{5,4},{6,7},{7,6},{8,9},{9,8},{10,11... | collective-permute-start | bytes 1966088 | tf_op jit(solution)/shard_map/ppermute | solution.py:218
  55.7 0.8 %copy-start.1 = (bf16[4,640,128]{2,1,0:T(8,128)(2,1)}, bf16[4,640,128]{2,1,0:T(8,128)(2,1)S(1)}, u32[]{:S(2)}) copy-start(bf16[4,640,128]{2,1,0:T(8,128)(2,1)S(1)} %collective-permute-done.other.kv) | copy-start | bytes 1966084
  64.7 11.8 %all-to-all-start.2 = ((bf16[8,32,128]{2,1,0:T(8,128)(2,1)}), bf16[8,32,128]{2,1,0:T(8,128)(2,1)S(1)}, u32[]{:S(2)}, u32[]{:S(2)}) async-start(bf16[8,32,128]{2,1,0:T(8,128)(2,1)} %attend_last.1), calls=%async_computation.2 | async-start | bytes 131072 | tf_op jit(solution)/shard_map/all_to_all | solution.py:240
  76.6 0.6 copy-start.2

commit v2 on v1

--- a/solution.py
+++ b/solution.py
@@ -1,4 +1,3 @@
-import functools
 import math
 
 import jax
@@ -8,6 +7,7 @@
 from jax.experimental.pallas import tpu as pltpu
 from jax.sharding import Mesh
 from jax.sharding import PartitionSpec as P
+
 
 HEADS = 8
 NODES = 128
@@ -25,8 +25,13 @@
 SCALE = math.log2(math.e) / math.sqrt(HEAD)
 VM = pl.BlockSpec(memory_space=pltpu.VMEM)
 SM = pl.BlockSpec(memory_space=pltpu.SMEM)
-KV_ROWS = 8 * 2 * HEAD
+KV = 2 * HEAD
+KV_ROWS = 8 * KV
 SENT_ROWS = KV_ROWS + 8 * 16
+RING = 8 * NODES
+Q_BLOCK = 256
+TOP_LANE = 48
+ROOM = pltpu.CompilerParams(vmem_limit_bytes=28 * 2**20)
 
 
 def iota(shape, dim):
@@ -72,7 +77,9 @@
         sent[h, 3 * HEAD :, :] = jnp.concatenate(parts, axis=0).astype(BF16)
 
 
-def repack_kernel(got, sent):
+def repack_kernel(got, sent, own):
+    for s in range(8):
+        own[s] = got[s, HEAD : 3 * HEAD, :]
     for chip in range(CHIPS):
         for s in range(8):
             sent[chip, s * 64 : (s + 1) * 64, :] = got[s, HEAD : 3 * HEAD, :]
@@ -81,45 +88,77 @@
             ]
 
 
-KEYS = CHIPS * 8 * NODES
-QUERIES = 8 * NODES
-Q_BLOCK = 256
-
-
-def load_operands(got, kv, q_s, k_s, v_s):
+def load_queries(got, q_s):
     for s in range(8):
         q_s[s * 128 : (s + 1) * 128, :] = got[s, 0:HEAD, :].T
-    for chip in range(CHIPS):
-        for s in range(8):
-            at = (chip * 8 + s) * 128
-            k_s[:, at : at + 128] = kv[chip, s * 64 : s * 64 + 32, :]
-            v_s[0:32, at : at + 128] = kv[chip, s * 64 + 32 : s * 64 + 64, :]
-    v_s[32:64, :] = jnp.ones((32, KEYS), BF16)
-
-
-def attend_first_kernel(got, kv, acc_out, max_out, q_s, k_s, v_s):
-    load_operands(got, kv, q_s, k_s, v_s)
-    for b in range(QUERIES // Q_BLOCK):
+
+
+def load_keys(pieces, k_s, v_s):
+    for at, piece in enumerate(pieces):
+        lanes = slice(at * 128, (at + 1) * 128)
+        k_s[:, lanes] = piece[:HEAD, :]
+        v_s[0:HEAD, lanes] = piece[HEAD:, :]
+    v_s[HEAD:, :] = jnp.ones((HEAD, v_s.shape[1]), BF16)
+
+
+def attend(q_s, k_s, v_s, before, after):
+    def scores_of(b):
+        return mm(q_s[b * Q_BLOCK : (b + 1) * Q_BLOCK, :], k_s[...])
+
+    blocks = RING // Q_BLOCK
+    scores = scores_of(0)
+    for b in range(blocks):
+        upcoming = scores_of(b + 1) if b + 1 < blocks else None
         at = slice(b * Q_BLOCK, (b + 1) * Q_BLOCK)
-        scores = mm(q_s[at, :], k_s[...])
         top = jnp.max(scores, axis=1, keepdims=True)
+        if before is not None:
+            old = before[at, TOP_LANE : TOP_LANE + 1]
+            top = jnp.maximum(old, top)
         weights = jnp.exp2(scores - top).astype(BF16)
-        acc_out[at, :] = mm(weights, v_s[...], ((1,), (1,)))
-        max_out[at, :] = jnp.broadcast_to(top, (Q_BLOCK, 128))
-
-
-def attend_last_kernel(got, kv, acc_in, max_in, out, q_s, k_s, v_s):
-    load_operands(got, kv, q_s, k_s, v_s)
-    for b in range(QUERIES // Q_BLOCK):
-        at = slice(b * Q_BLOCK, (b + 1) * Q_BLOCK)
-        scores = mm(q_s[at, :], k_s[...])
-        before = max_in[at, 0:1]
-        top = jnp.maximum(before, jnp.max(scores, axis=1, keepdims=True))
-        weights = jnp.exp2(scores - top).astype(BF16)
-        acc = acc_in[at, :] * jnp.exp2(before - top) + mm(weights, v_s[...], ((1,), (1,)))
-        done = (acc[:, 0:32] / acc[:, 32:33]).T.astype(BF16)
+        acc = mm(weights, v_s[...], ((1,), (1,)))
+        if before is not None:
+            acc = acc + before[at, :] * jnp.exp2(old - top)
+        after(b, at, acc, top)
+        scores = upcoming
+
+
+def keep(state_out):
+    def after(b, at, acc, top):
+        state_out[at, :] = jnp.where(iota(acc.shape, 1) < TOP_LANE, acc, top)
+
+    return after
+
+
+def attend_own_kernel(got, partner, state, q_s, k_s, v_s):
+    load_queries(got, q_s)
+    pieces = [got[s, HEAD : 3 * HEAD, :] for s in range(8)]
+    load_keys(pieces + [partner[s] for s in range(8)], k_s, v_s)
+    attend(q_s, k_s, v_s, None, keep(state))
+
+
+def load_near(place, got, kv, q_s, k_s, v_s):
+    load_queries(got, q_s)
+    pieces = []
+    for turn in range(1, CHIPS):
+        chip = (place[0] + turn) & (CHIPS - 1)
+        pieces += [kv[chip, s * KV : (s + 1) * KV, :] for s in range(8)]
+    load_keys(pieces, k_s, v_s)
+
+
+def attend_near_kernel(place, got, kv, before, state, q_s, k_s, v_s):
+    load_near(place, got, kv, q_s, k_s, v_s)
+    attend(q_s, k_s, v_s, before, keep(state))
+
+
+def attend_last_kernel(place, got, kv, before, out, q_s, k_s, v_s):
+    load_near(place, got, kv, q_s, k_s, v_s)
+
+    def after(b, at, acc, top):
+        done = (acc[:, :HEAD] / acc[:, HEAD : HEAD + 1]).T.astype(BF16)
         for i in range(Q_BLOCK // 128):
             out[b * (Q_BLOCK // 128) + i] = done[:, i * 128 : (i + 1) * 128]
+
+    attend(q_s, k_s, v_s, before, after)
 
 
 def edge_kernel(
@@ -197,8 +236,9 @@
     edge_dst,
     edge_count,
 ):
-    shape = jax.ShapeDtypeStruct
+    shape = pltpu.VMEM
     row = lambda v: v.reshape(1, WIDTH)
+    vmem = lambda v: pltpu.with_memory_space_constraint(v, pltpu.VMEM)
     normed, sent = pl.pallas_call(
         project_kernel,
         out_shape=(shape((NODES, WIDTH), BF16), shape((HEADS, 160, 128), BF16)),
@@ -207,36 +247,41 @@
         name="project",
     )(node_feats, row(norm_gain), w_query, w_key, w_value, jnp.swapaxes(send_list, 1, 2))
     got = lax.all_to_all(sent, HEAD_AXES, 0, 0, tiled=True)
-    shared = pl.pallas_call(
+    shared, own = pl.pallas_call(
         repack_kernel,
-        out_shape=shape((CHIPS, SENT_ROWS, 128), BF16),
+        out_shape=(shape((CHIPS, SENT_ROWS, 128), BF16), shape((8, KV, 128), BF16)),
         in_specs=[VM],
-        out_specs=VM,
+        out_specs=(VM, VM),
+        compiler_params=ROOM,
         name="repack",
-    )(got)
+    )(vmem(got))
     mine = lax.all_to_all(shared, CHIP_AXES, 0, 0, tiled=True)
+    partner = lax.ppermute(own, "core", [(0, 1), (1, 0)])
     other = lax.ppermute(mine, "core", [(0, 1), (1, 0)])
-    scratch = [
-        pltpu.VMEM((QUERIES, HEAD), BF16),
-        pltpu.VMEM((HEAD, KEYS), BF16),
-        pltpu.VMEM((2 * HEAD, KEYS), BF16),
-    ]
-    acc, top = pl.pallas_call(
-        attend_first_kernel,
-        out_shape=(shape((QUERIES, 64), F32), shape((QUERIES, 128), F32)),
-        in_specs=[VM] * 2,
-        out_specs=(VM, VM),
-        scratch_shapes=scratch,
-        name="attend_first",
-    )(got, mine)
-    attended = pl.pallas_call(
-        attend_last_kernel,
-        out_shape=shape((8, HEAD, NODES), BF16),
-        in_specs=[VM] * 4,
-        out_specs=VM,
-        scratch_shapes=scratch,
-        name="attend_last",
-    )(got, other, acc, top)
+    place = (lax.axis_index("yb") * 2 + lax.axis_index("zb")).reshape(1).astype(jnp.int32)
+
+    def attention(kernel, keys, out, *operands):
+        scratch = [
+            pltpu.VMEM((RING, HEAD), BF16),
+            pltpu.VMEM((HEAD, keys), BF16),
+            pltpu.VMEM((KV, keys), BF16),
+        ]
+        specs = [SM if v is place else VM for v in operands]
+        return pl.pallas_call(
+            kernel,
+            out_shape=out,
+            in_specs=specs,
+            out_specs=VM,
+            scratch_shapes=scratch,
+            compiler_params=ROOM,
+        )(*[v if v is place else vmem(v) for v in operands])
+
+    state = shape((RING, KV), F32)
+    held = attention(attend_own_kernel, 2 * RING, state, got, partner)
+    held = attention(attend_near_kernel, 3 * RING, state, place, got, mine, held)
+    attended = attention(
+        attend_last_kernel, 3 * RING, shape((8, HEAD, NODES), BF16), place, got, other, held
+    )
     back = lax.all_to_all(attended, HEAD_AXES, 0, 0, tiled=True)
     core = lax.axis_index("core").reshape(1).astype(jnp.int32)
     base = pl.pallas_call(
@@ -244,30 +289,32 @@
         out_shape=shape((NODES, WIDTH), F32),
         in_specs=[SM, SM] + [VM] * 12,
         out_specs=VM,
+        compiler_params=ROOM,
         name="edges",
     )(
         edge_count,
         core,
-        normed,
-        mine,
-        other,
+        vmem(normed),
+        vmem(mine),
+        vmem(other),
         send_count.T,
         edge_src,
         edge_dst,
-        msg_src_w,
-        msg_dst_w,
+        vmem(msg_src_w),
+        vmem(msg_dst_w),
         row(msg_bias),
-        msg_out_w,
+        vmem(msg_out_w),
         row(msg_out_bias),
         node_feats,
     )
     return pl.pallas_call(
         finish_kernel,
-        out_shape=shape((NODES, WIDTH), F32),
+        out_shape=jax.ShapeDtypeStruct((NODES, WIDTH), F32),
         in_specs=[VM] * 6,
         out_specs=VM,
+        compiler_params=ROOM,
         name="finish",
-    )(base, back, w_out, row(mlp_gain), mlp_up, mlp_down)
+    )(vmem(base), vmem(back), vmem(w_out), row(mlp_gain), vmem(mlp_up), vmem(mlp_down))
 
 
 def solution(mesh):
@@ -277,4 +324,5 @@
     rows = P(GRAPHS_DOM, None)
     blocks = P(GRAPHS_DOM, None, None)
     placed = (rows,) + (P(),) * 13 + (blocks, P("graphs", DOM), blocks, blocks, P(GRAPHS_DOM))
+
     return jax.shard_map(body, mesh=finer, in_specs=placed, out_specs=rows, check_vma=False)

time: 80.7 us -> 72.8 us (0.902)
  Pallas kernels: 27.4 us -> 16.4 us
  waiting for transfers between devices: 3.67 us -> 6.45 us
  starting transfers between devices: 8.75 us -> 11.3 us
  blocking collectives: 38 us -> 36.6 us
    pallas_call x4 -> x5, Pallas kernels: 20.8 us -> 12.7 us  [the longest x3 11.3 us: attention(): pl.pallas_call(kernel, out_shape=out, in_specs=specs, out_specs=VM, scrat...]
    pallas_call x1, Pallas kernels: 4.17 us -> 2.02 us  [body(): pl.pallas_call(edge_kernel, out_shape=shape((NODES, WIDTH), F32), in_spec...]
    ppermute x0 -> x1, starting transfers between devices: none -> 1.92 us  [body(): partner = lax.ppermute(own, 'core', [(0, 1), (1, 0)])]
    all_to_all x1, waiting for transfers between devices: 3.66 us -> 5.14 us  [body(): back = lax.all_to_all(attended, HEAD_AXES, 0, 0, tiled=True)]
    ppermute x0 -> x1, waiting for transfers between devices: none -> 1.31 us  [body(): partner = lax.ppermute(own, 'core', [(0, 1), (1, 0)])]
    all_to_all x1, blocking collectives: 10.8 us -> 9.79 us  [body(): mine = lax.all_to_all(shared, CHIP_AXES, 0, 0, tiled=True)]
  transfers between devices with their start and end apart: 2 -> 3, of which waited for: 1 -> 2; matrix products, arithmetic and copies ran while one was open for 0% -> 0% of each run, Pallas kernels for 15% -> 12%
where the time goes in v2:
time: 72.8 us; the launch traced here: 72.3 us
  blocking collectives  36.6 us (50%)
  Pallas kernels  16.4 us (23%)
  starting transfers between devices  11.3 us (16%)
  waiting for transfers between devices  6.45 us (9%)
  between operations  0.84 us (1%)
    all_to_all x1, blocking collectives, body(): got = lax.all_to_all(sent, HEAD_AXES, 0, 0, tiled=True)  26.8 us
    pallas_call x3, Pallas kernels, attention(): pl.pallas_call(kernel, out_shape=out, in_specs=specs, out_specs=VM, scrat...  11.3 us
    all_to_all x1, blocking collectives, body(): mine = lax.all_to_all(shared, CHIP_AXES, 0, 0, tiled=True)  9.79 us
    ppermute x1, starting transfers between devices, body(): other = lax.ppermute(mine, 'core', [(0, 1), (1, 0)])  5.4 us
    all_to_all x1, waiting for transfers between devices, body(): back = lax.all_to_all(attended, HEAD_AXES, 0, 0, tiled=True)  5.14 us
    all_to_all x1, starting transfers between devices, body(): back = lax.all_to_all(attended, HEAD_AXES, 0, 0, tiled=True)  4 us
    pallas_call x1, Pallas kernels, body(): pl.pallas_call(edge_kernel, out_shape=shape((NODES, WIDTH), F32), in_spec...  2.02 us
    ppermute x1, starting transfers between devices, body(): partner = lax.ppermute(own, 'core', [(0, 1), (1, 0)])  1.92 us
  transfers between devices with their start and end apart: 3, of which 2 were waited for; matrix products, arithmetic and copies ran while one was open for 0% of the time, Pallas kernels for 12%

profile of v2, /device:TPU:1, one launch (start us, length us, event | category | flops | bytes accessed | tf_op | source)
XLA Modules:
  0.0 72.3 jit_solution(4549475854221495877)
XLA Ops:
  0.0 1.7 %project.1 = (bf16[128,256]{1,0:T(8,128)(2,1)S(1)}, bf16[8,160,128]{2,1,0:T(8,128)(2,1)S(1)}) custom-call(f32[128,256]{1,0:T(8,128)} %feats.3, f32[1,256]{1,0:T(1,128)} %bitcast.13, bf16[256,256]{1,0:T(8,128)(2,1)} %wq.1, bf16[256,256]{1,0:T(8,128)(2,1)} %wk.1, bf16[256,256]{1,0:T(8,128)(2,1)} %wv.1, s32[1,4,64]{2,1,0:T(4,128)} %bitcast.12), custom_call_target="tpu_custom_call" | custom-call | tf_op jit(solution)/shard_map/project/pallas_call | solution.py:242
  1.7 26.8 %all_to_all.15.got = bf16[8,160,128]{2,1,0:T(8,128)(2,1)S(1)} all-to-all(bf16[8,160,128]{2,1,0:T(8,128)(2,1)S(1)} %get-tuple-element.10), channel_id=1, replica_groups=mesh['graphs'=8,'ya'=2,'yb'=2,'za'=4,'zb'=2,'core'=2] {'ya','za'}, dimensions={0} | all-to-all | bytes 655360 | tf_op jit(solution)/shard_map/all_to_all | solution.py:249
  28.5 0.1 repack.1
  28.6 9.8 %all_to_all.16.mine.kv = bf16[4,640,128]{2,1,0:T(8,128)(2,1)S(1)} all-to-all(bf16[4,640,128]{2,1,0:T(8,128)(2,1)S(1)} %get-tuple-element.11), channel_id=1, replica_groups=mesh['graphs'=8,'ya'=2,'yb'=2,'za'=4,'zb'=2,'core'=2] {'yb','zb'}, dimensions={0} | all-to-all | bytes 1310720 | tf_op jit(solution)/shard_map/all_to_all | solution.py:258
  38.4 5.4 %collective-permute-start = (bf16[4,640,128]{2,1,0:T(8,128)(2,1)S(1)}, bf16[4,640,128]{2,1,0:T(8,128)(2,1)S(1)}, u32[]{:S(2)}, u32[]{:S(2)}) collective-permute-start(bf16[4,640,128]{2,1,0:T(8,128)(2,1)S(1)} %all_to_all.16.mine.kv), channel_id=1, source_target_pairs={{0,1},{1,0},{2,3},{3,2},{4,5},{5,4},{6,7},{7,6},{8,9},{9,8},{10,11... | collective-permute-start | bytes 1966088 | tf_op jit(solution)/shard_map/ppermute | solution.py:260
  43.8 1.9 %collective-permute-start.1 = (bf16[8,64,128]{2,1,0:T(8,128)(2,1)S(1)}, bf16[8,64,128]{2,1,0:T(8,128)(2,1)S(1)}, u32[]{:S(2)}, u32[]{:S(2)}) collective-permute-start(bf16[8,64,128]{2,1,0:T(8,128)(2,1)S(1)} %get-tuple-element.12), channel_id=1, source_target_pairs={{0,1},{1,0},{2,3},{3,2},{4,5},{5,4},{6,7},{7,6},{8,9},{9,8},{10,11... | collective-permute-start | bytes 393224 | tf_op jit(solution)/shard_map/ppermute | solution.py:259
  45.7 1.3 %collective-permute-done.1.partner = bf16[8,64,128]{2,1,0:T(8,128)(2,1)S(1)} collective-permute-done((bf16[8,64,128]{2,1,0:T(8,128)(2,1)S(1)}, bf16[8,64,128]{2,1,0:T(8,128)(2,1)S(1)}, u32[]{:S(2)}, u32[]{:S(2)}) %collective-permute-start.1) | collective-permute-done | bytes 131104 | tf_op jit(solution)/shard_map/ppermute | solution.py:259
  47.0 2.6 %shard_map.181.before = f32[1024,64]{1,0:T(8,128)S(1)} custom-call(bf16[8,160,128]{2,1,0:T(8,128)(2,1)S(1)} %all_to_all.15.got, bf16[8,64,128]{2,1,0:T(8,128)(2,1)S(1)} %collective-permute-done.1.partner), custom_call_target="tpu_custom_call" | custom-call | tf_op jit(solution)/shard_map/pallas_call | solution.py:270
  49.7 3.9 %shard_map.182.before = f32[1024,64]{1,0:T(8,128)S(1)} custom-call(s32[1]{0:T(128)} %bitcast.6.place, bf16[8,160,128]{2,1,0:T(8,128)(2,1)S(1)} %all_to_all.15.got, bf16[4,640,128]{2,1,0:T(8,128)(2,1)S(1)} %all_to_all.16.mine.kv, f32[1024,64]{1,0:T(8,128)S(1)} %shard_map.181.before), custom_call_target="tpu_custom_call" | custom-call | tf_op jit(solution)/shard_map/pallas_call | solution.py:270
  53.6 0.0 collective-permute-done.other.kv
  53.6 0.0 copy-start.3
  53.6 0.0 copy-start.4
  53.6 0.0 copy-start.5
  53.6 4.7 %shard_map.183 = bf16[8,32,128]{2,1,0:T(8,128)(2,1)} custom-call(s32[1]{0:T(128)} %bitcast.6.place, bf16[8,160,128]{2,1,0:T(8,128)(2,1)S(1)} %all_to_all.15.got, bf16[4,640,128]{2,1,0:T(8,128)(2,1)S(1)} %collective-permute-done.other.kv, f32[1024,64]{1,0:T(8,128)S(1)} %shard_map.182.before), custom_call_target="tpu_custom_call" | custom-call | tf_op jit(solution)/shard_map/pallas_call | solution.py:270
  58.4 0.0 copy-start.2
  58.4 0.0 copy-start.10
  58.4 0.0 copy-start.12
  58.4 4.0 %all-to-all-start.2 = ((bf16[8,32,128]{2,1,0:T(8,128)(2,1)}), bf16[8,32,128]{2,1,0:T(8,128)(2,1)S(1)}, u32[]{:S(2)}, u32[]{:S(2)}) async-start(bf16[8,32,128]{2,1,0:T(8,128)(2,1)} %shard_map.183), calls=%async_computation.2 | async-start | bytes 131072 | tf_op jit(solution)/shard_map/all_to_all | solution.py:285
  63.0 0.0 copy-start.8
  63.0 0.0 copy-start.7
  63.1 0.0 copy-start.9
  63.1 0.0 copy-done.3
  63.1 0.0 copy-done.4
  63.1 0.0 copy-done.5
  63.1 0.0 copy-done.2
  63.1 0.0 copy-done.10
  63.1 0.0 copy-done.12
  63.1 0.6 copy-done.8
  63.7 0.0 copy-done.7
  63.7 0.0 copy-done.9
  63.7 0.0 copy-start
  63.7 0.0 copy-start.1
  63.7 0.0 copy-start.6
  63.8 2.0 %edges.1.base = f32[128,256]{1,0:T(8,128)S(1)} custom-call(s32[1]{0:T(128)S(6)} %copy.20.limit, s32[1]{0:T(128)} %bitcast.place, bf16[128,256]{1,0:T(8,128)(2,1)S(1)} %get-tuple-element.9.normed, bf16[4,640,128]{2,1,0:T(8,128)(2,1)S(1)} %all_to_all.16.mine.kv, bf16[4,640,128]{2,1,0:T(8,128)(2,1)S(1)} %collective-permute-done.other.kv, s32[1,64]{1,0:T(1,128)S(1)} %bitcast.11, ...), custom_call_target="tpu_custom_call" | custom-call | tf_op jit(solution)/shard_map/edges/pallas_call | solution.py:287
  65.8 0.0 copy-start.11
  65.8 5.1 %all-to-all-done.2.attended = bf16[8,32,128]{2,1,0:T(8,128)(2,1)S(1)} async-done(((bf16[8,32,128]{2,1,0:T(8,128)(2,1)}), bf16[8,32,128]{2,1,0:T(8,128)(2,1)S(1)}, u32[]{:S(2)}, u32[]{:S(2)}) %all-to-all-start.2) | async-done | bytes 65568 | tf_op jit(solution)/shard_map/all_to_all | solution.py:285
  70.9 0.0 copy-done
  70.9 0.0 copy-done.1
  70.9 0.0 copy-done.6
  70.9 0.0 copy-done.11
  71.0 1.4 %finish.1 = f32[128,256]{1,0:T(8,128)} custom-call(f32[128,256]{1,0:T(8,128)S(1)} %edges.1.base, bf16[8,32,128]{2,1,0:T(8,128)(2,1)S(1)} %all-to-all-done.2.attended, bf16[256,256]{1,0:T(8,128)(2,1)S(1)} %copy-done.6, f32[1,256]{1,0:T(1,128)S(1)} %bitcast.10, bf16[256,1024]{1,0:T(8,128)(2,1)S(1)} %copy-done, bf16[1024,256]{1,0:T(8,128)(2,1)S(1)} %copy-done.1), custom_call_target="tpu_custom_call" | custom-call | tf_op jit(solution)/shard_map/finish/pallas_call | solution.py:310
Async XLA Ops:
  38.4 15.2 %collective-permute-start = (bf16[4,640,128]{2,1,0:T(8,128)(2,1)S(1)}, bf16[4,640,128]{2,1,0:T(8,128)(2,1)S(1)}, u32[]{:S(2)}, u32[]{:S(2)}) collective-permute-start(bf16[4,640,128]{2,1,0:T(8,128)(2,1)S(1)} %all_to_all.16.mine.kv), channel_id=1, source_target_pairs={{0,1},{1,0},{2,3},{3,2},{4,5},{5,4},{6,7},{7,6},{8,9},{9,8},{10,11... | collective-permute-start | bytes 1966088 | tf_op jit(solution)/shard_map/ppermute | solution.py:260
  43.8 3.2 %collective-permute-start.1 = (bf16[8,64,128]{2,1,0:T(8,128)(2,1)S(1)}, bf16[8,64,128]{2,1,0:T(8,128)(2,1)S(1)}, u32[]{:S(2)}, u32[]{:S(2)}) collective-permute-start(bf16[8,64,128]{2,1,0:T(8,128)(2,1)S(1)} %get-tuple-element.12), channel_id=1, source_target_pairs={{0,1},{1,0},{2,3},{3,2},{4,5},{5,4},{6,7},{7,6},{8,9},{9,8},{10,11... | collective-permute-start | bytes 393224 | tf_op jit(solution)/shard_map/ppermute | solution.py:259
  53.6 9.5 %copy-start.3 = (bf16[256,256]{1,0:T(8,128)(2,1)S(1)}, bf16[256,256]{1,0:T(8,128)(2,1)}, u32[]{:S(2)}) copy-start(bf16[256,256]{1,0:T(8,128)(2,1)} %w_src.1) | copy-start | bytes 393220
  53.6 9.5 %copy-start.4 = (bf16[256,256]{1,0:T(8,128)(2,1)S(1)}, bf16[256,256]{1,0:T(8,128)(2,1)}, u32[]{:S(2)}) copy-start(bf16[256,256]{1,0:T(8,128)(2,1)} %w_dst.1) | copy-start | bytes 393220
  53.6 9.5 %copy-start.5 = (bf16[256,256]{1,0:T(8,128)(2,1)S(1)}, bf16[256,256]{1,0:T(8,128)(2,1)}, u32[]{:S(2)}) copy-start(bf16[256,256]{1,0:T(8,128)(2,1)} %w_out.2) | copy-start | bytes 393220
  58.4 4.7 %copy-start.2 = (f32[128,256]{1,0:T(8,128)S(1)}, f32[128,256]{1,0:T(8,128)}, u32[]{:S(2)}) copy-start(f32[128,256]{1,0:T(8,128)} %feats.3) | copy-start | bytes 393220
  58.4 4.7 %copy-start.10 = (f32[256]{0:T(256)S(1)}, f32[256]{0:T(256)}, u32[]{:S(2)}) copy-start(f32[256]{0:T(256)} %param.29) | copy-start | bytes 3076
  58.4 4.7 %copy-start.12 = (s32[64,1]{0,1:T(1,128)S(1)}, s32[64,1]{0,1:T(1,128)}, u32[]{:S(2)}) copy-start(s32[64,1]{0,1:T(1,128)} %param.34) | copy-start | bytes 772
  58.4 12.6 %all-to-all-start.2 = ((bf16[8,32,128]{2,1,0:T(8,128)(2,1)}), bf16[8,32,128]{2,1,0:T(8,128)(2,1)S(1)}, u32[]{:S(2)}, u32[]{:S(2)}) async-start(bf16[8,32,128]{2,1,0:T(8,128)(2,1)} %shard_map.183), calls=%async_computation.2 | async-start | bytes 131072 | tf_op jit(solution)/shard_map/all_to_all | solution.py:285
  63.0 0.7 copy-start.8
  63.0 0.7 copy-start.7
  63.1 0.7 copy-start.9
  63.7 7.2 %copy-start = (bf16[256,1024]{1,0:T(8,128)(2,1)S(1)}, bf16[256,1024]{1,0:T(8,128)(2,1)}, u32[]{:S(2)}) copy-start(bf16[256,1024]{1,0:T(8,128)(2,1)} %up.1) | copy-start | bytes 1572868
  63.7 7.2 %copy-start.1 = (bf16[1024,256]{1,0:T(8,128)(2,1)S(1)}, bf16[1024,256]{1,0:T(8,128)(2,1)}, u32[]{:S(2)}) copy-start(bf16[1024,256]{1,0:T(8,128)(2,1)} %down.1) | copy-start | bytes 1572868
  63.7 7.2 %copy-start.6 = (bf16[256,256]{1,0:T(8,128)(2,1)S(1)}, bf16[256,256]{1,0:T(8,128)(2,1)}, u32[]{:S(2)}) copy-start(bf16[256,256]{1,0:T(8,128)(2,1)} %w_out.3) | copy-start | bytes 393220
  65.8 5.2 %copy-start.11 = (f32[256]{0:T(256)S(1)}, f32[256]{0:T(256)}, u32[]{:S(2)}) copy-start(f32[256]{0:T(256)} %param.30) | copy-start | bytes 3076

commit v3 on v2

--- a/solution.py
+++ b/solution.py
@@ -17,9 +17,25 @@
 DOMS = 64
 DOM = ("ya", "yb", "za", "zb", "core")
 GRAPHS_DOM = ("graphs",) + DOM
-HEAD_AXES = ("ya", "za")
 CHIP_AXES = ("yb", "zb")
 CHIPS = 4
+FIRST = 3
+
+
+def block_of(j):
+    return (j >> 2) * 32 + ((j + FIRST) & 3) * 4
+
+
+def zb_of(j, group):
+    return group ^ (((j + FIRST) & 3) >> 1)
+
+
+HEAD_GROUPS = [
+    [block_of(j) + yb * 16 + zb_of(j, group) * 2 + core for j in range(8)]
+    for yb in range(2)
+    for group in range(2)
+    for core in range(2)
+]
 F32 = jnp.float32
 BF16 = jnp.bfloat16
 SCALE = math.log2(math.e) / math.sqrt(HEAD)
@@ -58,9 +74,8 @@
             sent[h, first : first + HEAD, :] = turned[h * HEAD : (h + 1) * HEAD, :]
     place = iota((DOMS * SLOTS, DOMS), 0)
     receiver = (
-        ((place >> 7) & 1) * 32
+        block_of(place >> 5)
         + ((place >> 4) & 1) * 16
-        + ((place >> 5) & 3) * 4
         + ((place >> 2) & 3)
     )
     pick_receiver = (receiver == iota((DOMS * SLOTS, DOMS), 1)).astype(BF16)
@@ -168,7 +183,7 @@
     tiles = src.shape[1]
     row = lambda ref: jnp.concatenate([ref[0, t : t + 1, :] for t in range(tiles)], axis=1)
     src_row, dst_row = row(src), row(dst)
-    core = place[0]
+    core, far = place[0], place[1]
     table = [normed[...].astype(F32)]
     for part in (mine, other):
         for chip in range(CHIPS):
@@ -180,9 +195,8 @@
     at = iota((total, 1), 0)
     sender_core = jnp.where(at >= 256, 1 - core, core)
     chip, s, to, slot = (at >> 6) & 3, (at >> 3) & 7, (at >> 2) & 1, at & 3
-    sender = (
-        (s >> 2) * 32 + (chip >> 1) * 16 + (s & 3) * 4 + (chip & 1) * 2 + sender_core
-    )
+    group = (chip & 1) ^ far
+    sender = block_of(s) + (chip >> 1) * 16 + zb_of(s, group) * 2 + sender_core
     wide = iota((total, DOMS), 1)
     held = jnp.broadcast_to(counts[...].astype(F32), (8, DOMS)).astype(BF16)
     count = mm((sender == wide).astype(BF16), held, ((1,), (1,)))[:, 0:1]
@@ -246,7 +260,9 @@
         out_specs=(VM, VM),
         name="project",
     )(node_feats, row(norm_gain), w_query, w_key, w_value, jnp.swapaxes(send_list, 1, 2))
-    got = lax.all_to_all(sent, HEAD_AXES, 0, 0, tiled=True)
+    got = lax.all_to_all(
+        sent, DOM, 0, 0, axis_index_groups=HEAD_GROUPS, tiled=True
+    )
     shared, own = pl.pallas_call(
         repack_kernel,
         out_shape=(shape((CHIPS, SENT_ROWS, 128), BF16), shape((8, KV, 128), BF16)),
@@ -282,8 +298,10 @@
     attended = attention(
         attend_last_kernel, 3 * RING, shape((8, HEAD, NODES), BF16), place, got, other, held
     )
-    back = lax.all_to_all(attended, HEAD_AXES, 0, 0, tiled=True)
-    core = lax.axis_index("core").reshape(1).astype(jnp.int32)
+    back = lax.all_to_all(
+        attended, DOM, 0, 0, axis_index_groups=HEAD_GROUPS, tiled=True
+    )
+    core = jnp.stack([lax.axis_index("core"), lax.axis_index("za") >> 1]).astype(jnp.int32)
     base = pl.pallas_call(
         edge_kernel,
         out_shape=shape((NODES, WIDTH), F32),

time: 72.8 us -> 69 us (0.948)
  waiting for transfers between devices: 6.45 us -> 2.67 us
  blocking collectives: 36.6 us -> 34.2 us
  starting transfers between devices: 11.3 us -> 13.1 us
    all_to_all x1, waiting for transfers between devices: 5.14 us -> 1.36 us  [body(): lax.all_to_all(attended, DOM, 0, 0, axis_index_groups=HEAD_GROUPS, tiled=...]
    all_to_all x1, blocking collectives: 26.8 us -> 23.8 us  [body(): lax.all_to_all(sent, DOM, 0, 0, axis_index_groups=HEAD_GROUPS, tiled=True)]
    all_to_all x1, starting transfers between devices: 4 us -> 6.4 us  [body(): lax.all_to_all(attended, DOM, 0, 0, axis_index_groups=HEAD_GROUPS, tiled=...]
  transfers between devices with their start and end apart: 3 -> 3, of which waited for: 2 -> 2; matrix products, arithmetic and copies ran while one was open for 0% -> 0% of each run, Pallas kernels for 12% -> 13%
where the time goes in v3:
time: 69 us; the launch traced here: 68.6 us
  blocking collectives  34.2 us (50%)
  Pallas kernels  17 us (25%)
  starting transfers between devices  13.1 us (19%)
  waiting for transfers between devices  2.67 us (4%)
  between operations  0.82 us (1%)
  local copies, waits for them, and re-layouts  0.7 us (1%)
    all_to_all x1, blocking collectives, body(): lax.all_to_all(sent, DOM, 0, 0, axis_index_groups=HEAD_GROUPS, tiled=True)  23.8 us
    pallas_call x3, Pallas kernels, attention(): pl.pallas_call(kernel, out_shape=out, in_specs=specs, out_specs=VM, scrat...  11.3 us
    all_to_all x1, blocking collectives, body(): mine = lax.all_to_all(shared, CHIP_AXES, 0, 0, tiled=True)  10.4 us
    all_to_all x1, starting transfers between devices, body(): lax.all_to_all(attended, DOM, 0, 0, axis_index_groups=HEAD_GROUPS, tiled=...  6.4 us
    ppermute x1, starting transfers between devices, body(): other = lax.ppermute(mine, 'core', [(0, 1), (1, 0)])  4.79 us
    pallas_call x1, Pallas kernels, body(): pl.pallas_call(edge_kernel, out_shape=shape((NODES, WIDTH), F32), in_spec...  2.59 us
    ppermute x1, starting transfers between devices, body(): partner = lax.ppermute(own, 'core', [(0, 1), (1, 0)])  1.92 us
    pallas_call x1, Pallas kernels, body(): pl.pallas_call(project_kernel, out_shape=(shape((NODES, WIDTH), BF16), sh...  1.66 us
  transfers between devices with their start and end apart: 3, of which 2 were waited for; matrix products, arithmetic and copies ran while one was open for 0% of the time, Pallas kernels for 13%

profile of v3, /device:TPU:1, one launch (start us, length us, event | category | flops | bytes accessed | tf_op | source)
XLA Modules:
  0.0 68.6 jit_solution(1801421323349515113)
XLA Ops:
  0.0 1.7 %project.1 = (bf16[128,256]{1,0:T(8,128)(2,1)S(1)}, bf16[8,160,128]{2,1,0:T(8,128)(2,1)S(1)}) custom-call(f32[128,256]{1,0:T(8,128)} %feats.3, f32[1,256]{1,0:T(1,128)} %bitcast.14, bf16[256,256]{1,0:T(8,128)(2,1)} %wq.1, bf16[256,256]{1,0:T(8,128)(2,1)} %wk.1, bf16[256,256]{1,0:T(8,128)(2,1)} %wv.1, s32[1,4,64]{2,1,0:T(4,128)} %bitcast.13), custom_call_target="tpu_custom_call" | custom-call | tf_op jit(solution)/shard_map/project/pallas_call | solution.py:256
  1.7 23.8 %all_to_all.15.got = bf16[8,160,128]{2,1,0:T(8,128)(2,1)S(1)} all-to-all(bf16[8,160,128]{2,1,0:T(8,128)(2,1)S(1)} %get-tuple-element.10), channel_id=1, replica_groups={{14,0,4,10,46,32,36,42},{15,1,5,11,47,33,37,43},{12,2,6,8,44,34,38,40},..., dimensions={0} | all-to-all | bytes 655360 | tf_op jit(solution)/shard_map/all_to_all | solution.py:263
  25.5 0.1 repack.1
  25.6 10.4 %all_to_all.16.mine.kv = bf16[4,640,128]{2,1,0:T(8,128)(2,1)S(1)} all-to-all(bf16[4,640,128]{2,1,0:T(8,128)(2,1)S(1)} %get-tuple-element.11), channel_id=1, replica_groups=mesh['graphs'=8,'ya'=2,'yb'=2,'za'=4,'zb'=2,'core'=2] {'yb','zb'}, dimensions={0} | all-to-all | bytes 1310720 | tf_op jit(solution)/shard_map/all_to_all | solution.py:274
  36.0 4.8 %collective-permute-start = (bf16[4,640,128]{2,1,0:T(8,128)(2,1)S(1)}, bf16[4,640,128]{2,1,0:T(8,128)(2,1)S(1)}, u32[]{:S(2)}, u32[]{:S(2)}) collective-permute-start(bf16[4,640,128]{2,1,0:T(8,128)(2,1)S(1)} %all_to_all.16.mine.kv), channel_id=1, source_target_pairs={{0,1},{1,0},{2,3},{3,2},{4,5},{5,4},{6,7},{7,6},{8,9},{9,8},{10,11... | collective-permute-start | bytes 1966088 | tf_op jit(solution)/shard_map/ppermute | solution.py:276
  40.8 1.9 %collective-permute-start.1 = (bf16[8,64,128]{2,1,0:T(8,128)(2,1)S(1)}, bf16[8,64,128]{2,1,0:T(8,128)(2,1)S(1)}, u32[]{:S(2)}, u32[]{:S(2)}) collective-permute-start(bf16[8,64,128]{2,1,0:T(8,128)(2,1)S(1)} %get-tuple-element.12), channel_id=1, source_target_pairs={{0,1},{1,0},{2,3},{3,2},{4,5},{5,4},{6,7},{7,6},{8,9},{9,8},{10,11... | collective-permute-start | bytes 393224 | tf_op jit(solution)/shard_map/ppermute | solution.py:275
  42.7 1.3 %collective-permute-done.1.partner = bf16[8,64,128]{2,1,0:T(8,128)(2,1)S(1)} collective-permute-done((bf16[8,64,128]{2,1,0:T(8,128)(2,1)S(1)}, bf16[8,64,128]{2,1,0:T(8,128)(2,1)S(1)}, u32[]{:S(2)}, u32[]{:S(2)}) %collective-permute-start.1) | collective-permute-done | bytes 131104 | tf_op jit(solution)/shard_map/ppermute | solution.py:275
  44.0 2.6 %shard_map.181.before = f32[1024,64]{1,0:T(8,128)S(1)} custom-call(bf16[8,160,128]{2,1,0:T(8,128)(2,1)S(1)} %all_to_all.15.got, bf16[8,64,128]{2,1,0:T(8,128)(2,1)S(1)} %collective-permute-done.1.partner), custom_call_target="tpu_custom_call" | custom-call | tf_op jit(solution)/shard_map/pallas_call | solution.py:286
  46.7 3.9 %shard_map.182.before = f32[1024,64]{1,0:T(8,128)S(1)} custom-call(s32[1]{0:T(128)} %bitcast.7.place, bf16[8,160,128]{2,1,0:T(8,128)(2,1)S(1)} %all_to_all.15.got, bf16[4,640,128]{2,1,0:T(8,128)(2,1)S(1)} %all_to_all.16.mine.kv, f32[1024,64]{1,0:T(8,128)S(1)} %shard_map.181.before), custom_call_target="tpu_custom_call" | custom-call | tf_op jit(solution)/shard_map/pallas_call | solution.py:286
  50.6 0.0 collective-permute-done.other.kv
  50.6 0.0 copy-start.3
  50.6 0.0 copy-start.4
  50.6 0.0 copy-start.5
  50.6 4.7 %shard_map.183 = bf16[8,32,128]{2,1,0:T(8,128)(2,1)} custom-call(s32[1]{0:T(128)} %bitcast.7.place, bf16[8,160,128]{2,1,0:T(8,128)(2,1)S(1)} %all_to_all.15.got, bf16[4,640,128]{2,1,0:T(8,128)(2,1)S(1)} %collective-permute-done.other.kv, f32[1024,64]{1,0:T(8,128)S(1)} %shard_map.182.before), custom_call_target="tpu_custom_call" | custom-call | tf_op jit(solution)/shard_map/pallas_call | solution.py:286
  55.4 0.0 copy-start.2
  55.4 0.0 copy-start.10
  55.4 0.0 copy-start.12
  55.4 6.4 %all-to-all-start.2 = ((bf16[8,32,128]{2,1,0:T(8,128)(2,1)}), bf16[8,32,128]{2,1,0:T(8,128)(2,1)S(1)}, u32[]{:S(2)}, u32[]{:S(2)}) async-start(bf16[8,32,128]{2,1,0:T(8,128)(2,1)} %shard_map.183), calls=%async_computation.2 | async-start | bytes 131072 | tf_op jit(solution)/shard_map/all_to_all | solution.py:301
  62.4 0.0 copy-start.8
  62.5 0.1 pad_add_fusion.place
  62.5 0.0 copy-start.7
  62.5 0.0 copy-start.9
  62.5 0.0 copy-done.3
  62.5 0.0 copy-done.4
  62.5 0.0 copy-done.5
  62.6 0.0 copy-done.2
  62.6 0.0 copy-done.10
  62.6 0.0 copy-done.12
  62.6 0.5 copy-done.8
  63.1 0.1 copy-done.7
  63.2 0.0 copy-done.9
  63.2 0.0 copy-start
  63.2 0.0 copy-start.1
  63.2 0.0 copy-start.6
  63.2 2.6 %edges.1.base = f32[128,256]{1,0:T(8,128)S(1)} custom-call(s32[1]{0:T(128)S(6)} %copy.20.limit, s32[2]{0:T(128)S(1)} %pad_add_fusion.place, bf16[128,256]{1,0:T(8,128)(2,1)S(1)} %get-tuple-element.9.normed, bf16[4,640,128]{2,1,0:T(8,128)(2,1)S(1)} %all_to_all.16.mine.kv, bf16[4,640,128]{2,1,0:T(8,128)(2,1)S(1)} %collective-permute-done.other.kv, ...), custom_call_target="tpu_custom_call" | custom-call | tf_op jit(solution)/shard_map/edges/pallas_call | solution.py:305
  65.8 0.0 copy-start.11
  65.8 1.4 %all-to-all-done.2.attended = bf16[8,32,128]{2,1,0:T(8,128)(2,1)S(1)} async-done(((bf16[8,32,128]{2,1,0:T(8,128)(2,1)}), bf16[8,32,128]{2,1,0:T(8,128)(2,1)S(1)}, u32[]{:S(2)}, u32[]{:S(2)}) %all-to-all-start.2) | async-done | bytes 65568 | tf_op jit(solution)/shard_map/all_to_all | solution.py:301
  67.2 0.0 copy-done
  67.2 0.0 copy-done.1
  67.2 0.0 copy-done.6
  67.2 0.0 copy-done.11
  67.2 1.4 %finish.1 = f32[128,256]{1,0:T(8,128)} custom-call(f32[128,256]{1,0:T(8,128)S(1)} %edges.1.base, bf16[8,32,128]{2,1,0:T(8,128)(2,1)S(1)} %all-to-all-done.2.attended, bf16[256,256]{1,0:T(8,128)(2,1)S(1)} %copy-done.6, f32[1,256]{1,0:T(1,128)S(1)} %bitcast.11, bf16[256,1024]{1,0:T(8,128)(2,1)S(1)} %copy-done, bf16[1024,256]{1,0:T(8,128)(2,1)S(1)} %copy-done.1), custom_call_target="tpu_custom_call" | custom-call | tf_op jit(solution)/shard_map/finish/pallas_call | solution.py:328
Async XLA Ops:
  36.0 14.6 %collective-permute-start = (bf16[4,640,128]{2,1,0:T(8,128)(2,1)S(1)}, bf16[4,640,128]{2,1,0:T(8,128)(2,1)S(1)}, u32[]{:S(2)}, u32[]{:S(2)}) collective-permute-start(bf16[4,640,128]{2,1,0:T(8,128)(2,1)S(1)} %all_to_all.16.mine.kv), channel_id=1, source_target_pairs={{0,1},{1,0},{2,3},{3,2},{4,5},{5,4},{6,7},{7,6},{8,9},{9,8},{10,11... | collective-permute-start | bytes 1966088 | tf_op jit(solution)/shard_map/ppermute | solution.py:276
  40.8 3.2 %collective-permute-start.1 = (bf16[8,64,128]{2,1,0:T(8,128)(2,1)S(1)}, bf16[8,64,128]{2,1,0:T(8,128)(2,1)S(1)}, u32[]{:S(2)}, u32[]{:S(2)}) collective-permute-start(bf16[8,64,128]{2,1,0:T(8,128)(2,1)S(1)} %get-tuple-element.12), channel_id=1, source_target_pairs={{0,1},{1,0},{2,3},{3,2},{4,5},{5,4},{6,7},{7,6},{8,9},{9,8},{10,11... | collective-permute-start | bytes 393224 | tf_op jit(solution)/shard_map/ppermute | solution.py:275
  50.6 11.9 %copy-start.3 = (bf16[256,256]{1,0:T(8,128)(2,1)S(1)}, bf16[256,256]{1,0:T(8,128)(2,1)}, u32[]{:S(2)}) copy-start(bf16[256,256]{1,0:T(8,128)(2,1)} %w_src.1) | copy-start | bytes 393220
  50.6 11.9 %copy-start.4 = (bf16[256,256]{1,0:T(8,128)(2,1)S(1)}, bf16[256,256]{1,0:T(8,128)(2,1)}, u32[]{:S(2)}) copy-start(bf16[256,256]{1,0:T(8,128)(2,1)} %w_dst.1) | copy-start | bytes 393220
  50.6 11.9 %copy-start.5 = (bf16[256,256]{1,0:T(8,128)(2,1)S(1)}, bf16[256,256]{1,0:T(8,128)(2,1)}, u32[]{:S(2)}) copy-start(bf16[256,256]{1,0:T(8,128)(2,1)} %w_out.2) | copy-start | bytes 393220
  55.4 7.2 %copy-start.2 = (f32[128,256]{1,0:T(8,128)S(1)}, f32[128,256]{1,0:T(8,128)}, u32[]{:S(2)}) copy-start(f32[128,256]{1,0:T(8,128)} %feats.3) | copy-start | bytes 393220
  55.4 7.2 %copy-start.10 = (f32[256]{0:T(256)S(1)}, f32[256]{0:T(256)}, u32[]{:S(2)}) copy-start(f32[256]{0:T(256)} %param.29) | copy-start | bytes 3076
  55.4 7.2 %copy-start.12 = (s32[64,1]{0,1:T(1,128)S(1)}, s32[64,1]{0,1:T(1,128)}, u32[]{:S(2)}) copy-start(s32[64,1]{0,1:T(1,128)} %param.34) | copy-start | bytes 772
  55.4 11.8 %all-to-all-start.2 = ((bf16[8,32,128]{2,1,0:T(8,128)(2,1)}), bf16[8,32,128]{2,1,0:T(8,128)(2,1)S(1)}, u32[]{:S(2)}, u32[]{:S(2)}) async-start(bf16[8,32,128]{2,1,0:T(8,128)(2,1)} %shard_map.183), calls=%async_computation.2 | async-start | bytes 131072 | tf_op jit(solution)/shard_map/all_to_all | solution.py:301
  62.4 0.7 %copy-start.8 = (s32[1,8,128]{2,1,0:T(8,128)S(1)}, s32[1,8,128]{2,1,0:T(8,128)}, u32[]{:S(2)}) copy-start(s32[1,8,128]{2,1,0:T(8,128)} %dst.1) | copy-start | bytes 12292
  62.5 0.7 %copy-start.7 = (s32[1,8,128]{2,1,0:T(8,128)S(1)}, s32[1,8,128]{2,1,0:T(8,128)}, u32[]{:S(2)}) copy-start(s32[1,8,128]{2,1,0:T(8,128)} %src.1) | copy-start | bytes 12292
  62.5 0.7 %copy-start.9 = (f32[256]{0:T(256)S(1)}, f32[256]{0:T(256)}, u32[]{:S(2)}) copy-start(f32[256]{0:T(256)} %param.27) | copy-start | bytes 3076
  63.2 4.0 %copy-start = (bf16[256,1024]{1,0:T(8,128)(2,1)S(1)}, bf16[256,1024]{1,0:T(8,128)(2,1)}, u32[]{:S(2)}) copy-start(bf16[256,1024]{1,0:T(8,128)(2,1)} %up.1) | copy-start | bytes 1572868
  63.2 4.0 %copy-start.1 = (bf16[1024,256]{1,0:T(8,128)(2,1)S(1)}, bf16[1024,256]{1,0:T(8,128)(2,1)}, u32[]{:S(2)}) copy-start(bf16[1024,256]{1,0:T(8,128)(2,1)} %down.1) | copy-start | bytes 1572868
  63.2 4.0 %copy-start.6 = (bf16[256,256]{1,0:T(8,128)(2,1)S(1)}, bf16[256,256]{1,0:T(8,128)(2,1)}, u32[]{:S(2)}) copy-start(bf16[256,256]{1,0:T(8,128)(2,1)} %w_out.3) | copy-start | bytes 393220
  65.8 1.4 %copy-start.11 = (f32[256]{0:T(256)S(1)}, f32[256]{0:T(256)}, u32[]{:S(2)}) copy-start(f32[256]{0:T(256)} %param.30) | copy-start | bytes 3076
